TPU v7x, 32 devices: a whole 2x2x4 slice. The times are simulated.
32 devices in a mesh: nodes: 16 (over z, y, x), feat: 2 (over core).
Axes of the slice: x: 2, y: 2, z: 4, core: 2. Of those that a mesh axis runs over, the one named last changes fastest.
Arguments:
- grid_latent: bfloat16 [16384, 512], P('nodes', 'feat'), may hold values from -6 to 6
- mesh_latent: bfloat16 [16384, 512], P('nodes', 'feat'), may hold values from -6 to 6
- grid_order: int32 [16, 1024], P('nodes'), may hold values from 0 to 1023, each once within a row
- enc_send_block: int32 [256], P('nodes'), may hold values from 0 to 7
- enc_recv_block: int32 [256], P('nodes'), may hold values from 0 to 7
- enc_offsets: int32 [256, 2, 128], P('nodes'), may hold values from 0 to 127
- enc_classes: int32 [256, 128], P('nodes'), may hold values from 0 to 7
- enc_live: int32 [16], P('nodes'), may hold values from 1 to 16, 160 in all
- mesh_send_block: int32 [1536], P('nodes'), may hold values from 0 to 23
- mesh_recv_block: int32 [1536], P('nodes'), may hold values from 0 to 7
- mesh_offsets: int32 [1536, 2, 128], P('nodes'), may hold values from 0 to 127
- mesh_classes: int32 [1536, 128], P('nodes'), may hold values from 0 to 7
- mesh_live: int32 [16], P('nodes'), may hold values from 1 to 96, 960 in all
- dec_send_block: int32 [384], P('nodes'), may hold values from 0 to 7
- dec_recv_block: int32 [384], P('nodes'), may hold values from 0 to 7
- dec_offsets: int32 [384, 2, 128], P('nodes'), may hold values from 0 to 127
- dec_classes: int32 [384, 128], P('nodes'), may hold values from 0 to 7
- dec_live: int32 [16], P('nodes'), may hold values from 1 to 24, 240 in all
- class_gain: float32 [3, 8], replicated, may hold values from 0.25 to 2
- enc_weights: bfloat16 [3, 512, 512], P(None, None, 'feat'), may hold values from -0.25 to 0.25
- mesh_weights: bfloat16 [2, 3, 512, 512], P(None, None, None, 'feat'), may hold values from -0.25 to 0.25
- dec_weights: bfloat16 [3, 512, 512], P(None, None, 'feat'), may hold values from -0.25 to 0.25
- enc_bias: float32 [512], P('feat'), may hold values from -3 to 3
- enc_gain: float32 [512], P('feat'), may hold values from 0.25 to 1.75
- mesh_bias: float32 [2, 512], P(None, 'feat'), may hold values from -3 to 3
- mesh_gain: float32 [2, 512], P(None, 'feat'), may hold values from 0.25 to 1.75
- dec_bias: float32 [512], P('feat'), may hold values from -3 to 3
- dec_gain: float32 [512], P('feat'), may hold values from 0.25 to 1.75
Outputs:
- grid_out: bfloat16 [16384, 512], P('nodes', 'feat')
- mesh_final: bfloat16 [16384, 512], P('nodes', 'feat')
Inputs may be any that keep to these rules, and one draw needn't show every extreme that they name: Each row of grid_order lists each of 0..1023 once. The first enc_live[d] edge blocks of region d are live; the most is reached on some region. The first mesh_live[d] edge blocks of region d are live; the most is reached on some region. The first dec_live[d] edge blocks of region d are live; the most is reached on some region.
All inputs are finite; a program needn't handle non-finite values.
Results may differ from a plain program's by a relative error of at most 0.0085.
Values may be sent and summed in bfloat16 or wider, within the bound.
No kernel may reach another device: no remote copies, remote signals or barrier semaphores. Data moves between devices by JAX's collectives and lax.ppermute only.
A program may use at most 64 MiB of HBM per device.

v0:
```python
import functools
import math

import jax
import jax.numpy as jnp
from jax import lax
from jax.experimental import pallas as pl
from jax.experimental.pallas import tpu as pltpu
from jax.sharding import PartitionSpec as P


BLOCK = 128
ROUNDS = 2
UNROLL = 4
CHUNKS = 4
EPSILON = 1e-05

VMEM = pl.BlockSpec(memory_space=pltpu.VMEM)
SMEM = pl.BlockSpec(memory_space=pltpu.SMEM)
HBM = pl.BlockSpec(memory_space=pltpu.HBM)
F32 = jnp.float32
BF16 = jnp.bfloat16


def dot(a, b):
    return jnp.dot(a, b, preferred_element_type=F32)


def params(mib=24):
    return pltpu.CompilerParams(vmem_limit_bytes=mib << 20)


def pieces(rows):
    return min(rows, 256)


def entry(slot, sender, taker, total):
    return slot + sender * 256 + taker * 65536 + total * 16777216


def list_length(slots):
    return slots + 2 * UNROLL


def own_parts(chunks):
    return max(chunks - 1, 1)


def spread_weights(labels, gains, index):
    marks = labels[...]
    weight = jnp.zeros(marks.shape, F32)
    for k in range(gains.shape[1]):
        weight = jnp.where(marks == k, gains[index, k], weight)
    return weight


def prepare_kernel(blocks, chunks, parity, *refs):
    inputs, refs = refs[:13], refs[13:]
    (e_list, m_list, d_list, counts, e_w, m_w, d_w), refs = refs[:7], refs[7:]
    held, sems = refs[:13], refs[13]
    copies = [
        pltpu.make_async_copy(source, target, sems.at[k])
        for k, (source, target) in enumerate(zip(inputs, held))
    ]
    for copy in copies:
        copy.start()
    for copy in copies:
        copy.wait()
    gains, es, er, el, ec, ms, mr, ml, mc, ds, dr, dl, dc = held

    def finish(out, base, count):
        for k in range(2 * UNROLL):
            out[base + count + k] = entry(0, 0, 0, blocks)
        return jnp.maximum((count + UNROLL - 1) // UNROLL, 1)

    def plain(sends, takes, live, out, where):
        total = live[0]

        def step(i, carry):
            taker = takes[i]
            out[i] = entry(i, sends[i], taker, taker)
            return carry

        lax.fori_loop(0, total, step, 0)
        counts[where] = finish(out, 0, total)

    plain(es, er, el, e_list, 0)
    plain(ds, dr, dl, d_list, 1)
    length = list_length(ms.shape[0])
    first = jnp.where(parity[0] == 0, 2, 0)
    last = 2 - first
    per = blocks // chunks

    def step(i, carry):
        sender = ms[i]
        taker = mr[i]
        group = sender // blocks
        inner = sender - group * blocks
        late = inner >= blocks - per
        inner = jnp.where((group == last) & late, inner - (blocks - per), inner)
        turn = carry[-1]
        which = jnp.where(
            group == 1, 3 + turn, jnp.where(group == first, 0, jnp.where(late, 2, 1))
        )
        place = carry[0]
        for k in range(1, lists):
            place = jnp.where(which == k, length * k + carry[k], place)
        m_list[place] = entry(i, inner, taker, taker)
        turn = jnp.where(group == 1, turn + 1, turn)
        turn = jnp.where(turn == lists - 3, 0, turn)
        counted = [c + (which == k).astype(jnp.int32) for k, c in enumerate(carry[:-1])]
        return (*counted, turn)

    lists = 3 + own_parts(chunks)
    zero = tuple(jnp.int32(0) for _ in range(lists + 1))
    found = lax.fori_loop(0, ml[0], step, zero)
    for k, count in enumerate(found[:-1]):
        counts[2 + k] = finish(m_list, length * k, count)

    for index, (labels, out) in enumerate(((ec, e_w), (mc, m_w), (dc, d_w))):
        out[...] = spread_weights(labels, gains, index)


def prepare(blocks, chunks, parity, gains, enc, mesh, dec):
    i32 = jnp.int32
    sets = (enc, mesh, dec)
    slots = [s[0].shape[0] for s in sets]
    sizes = [list_length(slots[0]), (3 + own_parts(chunks)) * list_length(slots[1])]
    sizes += [list_length(slots[2]), 8 + chunks]
    out_shape = [jax.ShapeDtypeStruct((n,), i32) for n in sizes]
    out_shape += [jax.ShapeDtypeStruct((n, BLOCK), F32) for n in slots]
    arrays = [gains, *enc, *mesh, *dec]
    spaces = [pltpu.SMEM] + [pltpu.SMEM, pltpu.SMEM, pltpu.SMEM, pltpu.VMEM] * 3
    scratch = [space(x.shape, x.dtype) for space, x in zip(spaces, arrays)]
    scratch.append(pltpu.SemaphoreType.DMA((len(arrays),)))
    return pl.pallas_call(
        functools.partial(prepare_kernel, blocks, chunks),
        out_shape=out_shape,
        in_specs=[SMEM] + [HBM] * len(arrays),
        out_specs=[SMEM] * 4 + [VMEM] * 3,
        scratch_shapes=scratch,
        compiler_params=params(4),
        cost_estimate=pl.CostEstimate(
            flops=2_000_000_000, bytes_accessed=1_000_000, transcendentals=0
        ),
    )(parity, *arrays)


def edge_loop(base, trips, items, send, take, offsets, weights, acc, picks, held):
    rows = lax.broadcasted_iota(jnp.int32, (BLOCK, BLOCK), 0).astype(F32).astype(BF16)
    one = jnp.ones((BLOCK, BLOCK), BF16)
    nil = jnp.zeros((BLOCK, BLOCK), BF16)

    def spread(row):
        return jnp.broadcast_to(row.astype(F32).astype(BF16), (BLOCK, BLOCK))

    def build(i):
        for u in range(UNROLL):
            slot = items[base + i * UNROLL + u] & 255
            both = [
                jnp.where(rows == spread(offsets[pl.ds(2 * slot + k, 1), :]), one, nil)
                for k in range(2)
            ]
            picks[u] = jnp.concatenate([x.T for x in both], axis=1)

    def gather(i):
        for u in range(UNROLL):
            item = items[base + i * UNROLL + u]
            sender = pl.multiple_of(((item >> 8) & 255) * BLOCK, BLOCK)
            taker = pl.multiple_of(((item >> 16) & 255) * BLOCK, BLOCK)
            both = jnp.concatenate(
                [send[pl.ds(sender, BLOCK), :], take[pl.ds(taker, BLOCK), :]], axis=0
            )
            half = dot(picks[u], both)
            held[u] = (half + half * jnp.tanh(half)).astype(BF16)

    def scatter(i):
        for u in range(UNROLL):
            item = items[base + i * UNROLL + u]
            slot = item & 255
            total = pl.multiple_of((item >> 24) * BLOCK, BLOCK)
            is_to = rows == spread(offsets[pl.ds(2 * slot + 1, 1), :])
            put = jnp.where(is_to, spread(weights[pl.ds(slot, 1), :]), nil)
            acc[pl.ds(total, BLOCK), :] += dot(put, held[u])

    def turn(i, carry):
        scatter(i - 1)
        gather(i)
        build(i + 1)
        return carry

    build(0)
    gather(0)
    build(1)
    lax.fori_loop(1, trips, turn, 0)
    scatter(trips - 1)


def edge_kernel(where, base, pieces_in, first, last, counts, items, *refs):
    refs = list(refs)
    sends = [refs.pop(0) for _ in range(pieces_in)]
    take, offsets, weights = refs[:3]
    refs = refs[3:]
    if not first:
        before = refs.pop(0)
    out, picks, held = refs[:3]
    refs = refs[3:]
    acc = refs.pop(0) if last else out
    if first:
        acc[...] = jnp.zeros_like(acc)
    elif last:
        acc[...] = before[...]
    send = sends[0]
    if pieces_in > 1:
        joined = refs.pop(0)
        depth = send.shape[0]
        for k, piece in enumerate(sends):
            joined[pl.ds(k * depth, depth), :] = piece[...]
        send = joined
    edge_loop(base, counts[where], items, send, take, offsets, weights, acc, picks, held)
    if last:
        out[...] = acc[pl.ds(0, out.shape[0]), :].astype(out.dtype)


def edge_sum(where, base, counts, items, sends, take, offsets, weights, before, last):
    first = before is None
    rows, columns = take.shape
    arrays = [counts, items, *sends, take, offsets, weights]
    aliases = {}
    if not first:
        if not last:
            aliases = {len(arrays): 0}
        arrays.append(before)
    full = (rows + BLOCK, columns)
    scratch = [
        pltpu.VMEM((UNROLL, BLOCK, width), BF16) for width in (2 * BLOCK, columns)
    ]
    if last:
        scratch.append(pltpu.VMEM(full, F32))
        shape = jax.ShapeDtypeStruct((rows, columns), BF16)
    else:
        shape = jax.ShapeDtypeStruct(full, F32)
    if len(sends) > 1:
        depth = sum(x.shape[0] for x in sends)
        scratch.append(pltpu.VMEM((depth, columns), BF16))
    return pl.pallas_call(
        functools.partial(edge_kernel, where, base, len(sends), first, last),
        out_shape=shape,
        in_specs=[SMEM, SMEM] + [VMEM] * (len(arrays) - 2),
        out_specs=VMEM,
        scratch_shapes=scratch,
        input_output_aliases=aliases,
        compiler_params=params(),
        cost_estimate=pl.CostEstimate(
            flops=2_000_000_000, bytes_accessed=2_000_000, transcendentals=1_000_000
        ),
    )(*arrays)


def two_dots(a, b, weights, mine, other, width):
    return dot(a, weights[pl.ds(mine, width), :]) + dot(b, weights[pl.ds(other, width), :])


def normalized(ym, yt):
    width = ym.shape[1] + yt.shape[1]
    total = jnp.sum(ym + yt, axis=1, keepdims=True)
    squares = jnp.sum(ym * ym + yt * yt, axis=1, keepdims=True)
    mean = total / width
    spread = squares / width - mean * mean
    return mean, lax.rsqrt(spread + EPSILON)


def mix_kernel(
    core, am, at, xm, xt, wm, wt, gm, gt, ws, out_m, out_t, out_s
):
    rows, width = am.shape
    tile = pieces(rows)
    mine = pl.multiple_of(core[0] * width, width)
    other = pl.multiple_of(width - core[0] * width, width)

    for t in range(rows // tile):
        part = pl.ds(t * tile, tile)
        a = am[part, :]
        b = at[part, :]
        ym = two_dots(a, b, wm, mine, other, width)
        yt = two_dots(a, b, wt, mine, other, width)
        mean, scale = normalized(ym, yt)
        nm = (xm[part, :].astype(F32) + (ym - mean) * scale * gm[...]).astype(BF16)
        nt = (xt[part, :].astype(F32) + (yt - mean) * scale * gt[...]).astype(BF16)
        out_m[part, :] = nm
        out_t[part, :] = nt
        out_s[part, :] = (0.5 * two_dots(nm, nt, ws, mine, other, width)).astype(BF16)


def mix(core, am, at, xm, xt, wm, wt, gm, gt, ws):
    shape = jax.ShapeDtypeStruct(am.shape, BF16)
    return pl.pallas_call(
        mix_kernel,
        out_shape=[shape] * 3,
        in_specs=[SMEM] + [VMEM] * 9,
        out_specs=[VMEM] * 3,
        compiler_params=params(),
    )(core, am, at, xm, xt, wm, wt, gm, gt, ws)


def project_kernel(core, xm, xt, w, bias, out):
    rows, width = xm.shape
    tile = pieces(rows)
    mine = pl.multiple_of(core[0] * width, width)
    other = pl.multiple_of(width - core[0] * width, width)

    for t in range(rows // tile):
        part = pl.ds(t * tile, tile)
        y = two_dots(xm[part, :], xt[part, :], w, mine, other, width)
        out[part, :] = (0.5 * (y + bias[...])).astype(BF16)


def project(core, xm, xt, w, bias):
    return pl.pallas_call(
        project_kernel,
        out_shape=jax.ShapeDtypeStruct(xm.shape, BF16),
        in_specs=[SMEM] + [VMEM] * 4,
        out_specs=VMEM,
        compiler_params=params(),
    )(core, xm, xt, w, bias)


def update_kernel(core, am, at, wm, wt, gm, out):
    rows, width = am.shape
    tile = pieces(rows)
    mine = pl.multiple_of(core[0] * width, width)
    other = pl.multiple_of(width - core[0] * width, width)

    for t in range(rows // tile):
        part = pl.ds(t * tile, tile)
        a = am[part, :]
        b = at[part, :]
        ym = two_dots(a, b, wm, mine, other, width)
        yt = two_dots(a, b, wt, mine, other, width)
        mean, scale = normalized(ym, yt)
        out[part, :] = ((ym - mean) * scale * gm[...]).astype(BF16)


def update_of(core, am, at, wm, wt, gm):
    return pl.pallas_call(
        update_kernel,
        out_shape=jax.ShapeDtypeStruct(am.shape, BF16),
        in_specs=[SMEM] + [VMEM] * 5,
        out_specs=VMEM,
        compiler_params=params(),
    )(core, am, at, wm, wt, gm)


def pick_rows_kernel(order_in, x_in, out, order, x, sems):
    copies = [
        pltpu.make_async_copy(order_in, order, sems.at[0]),
        pltpu.make_async_copy(x_in, x, sems.at[1]),
    ]
    for copy in copies:
        copy.start()
    for copy in copies:
        copy.wait()
    rows = x.shape[0]
    tile = pieces(rows)
    for t in range(rows // tile):
        part = pl.ds(t * tile, tile)
        ids = lax.broadcasted_iota(jnp.int32, (rows, tile), 0)
        chosen = jnp.where(ids == order[:, part], 1.0, 0.0).astype(BF16)
        out[part, :] = lax.dot_general(
            chosen, x[...], (((0,), (0,)), ((), ())), preferred_element_type=F32
        ).astype(BF16)


def pick_rows(order, x):
    return pl.pallas_call(
        pick_rows_kernel,
        out_shape=jax.ShapeDtypeStruct(x.shape, BF16),
        in_specs=[HBM] * 2,
        out_specs=VMEM,
        scratch_shapes=[
            pltpu.VMEM(order.shape, order.dtype),
            pltpu.VMEM(x.shape, x.dtype),
            pltpu.SemaphoreType.DMA((2,)),
        ],
        compiler_params=params(62),
    )(order, x)


def place_rows_kernel(order, x, rest, out):
    rows = x.shape[0]
    tile = pieces(rows)

    for t in range(rows // tile):
        start = t * tile
        part = pl.ds(start, tile)
        ids = lax.broadcasted_iota(jnp.int32, (tile, rows), 0) + start
        chosen = jnp.where(ids == order[...], 1.0, 0.0).astype(BF16)
        out[part, :] = (rest[part, :].astype(F32) + dot(chosen, x[...])).astype(BF16)


def place_rows(order, x, rest):
    return pl.pallas_call(
        place_rows_kernel,
        out_shape=jax.ShapeDtypeStruct(x.shape, BF16),
        in_specs=[VMEM] * 3,
        out_specs=VMEM,
        compiler_params=params(),
    )(order, x, rest)


def swap(x):
    return lax.ppermute(x, "feat", [(0, 1), (1, 0)])


def exchange(x):
    return lax.all_to_all(x, "nodes", split_axis=0, concat_axis=0, tiled=True)


def tie(*values):
    return lax.optimization_barrier(values)


def ring(chunk, pairs):
    return lax.ppermute(chunk, "nodes", pairs)


def local(
    grid_latent,
    mesh_latent,
    grid_order,
    enc_send_block,
    enc_recv_block,
    enc_offsets,
    enc_classes,
    enc_live,
    mesh_send_block,
    mesh_recv_block,
    mesh_offsets,
    mesh_classes,
    mesh_live,
    dec_send_block,
    dec_recv_block,
    dec_offsets,
    dec_classes,
    dec_live,
    class_gain,
    enc_weights,
    mesh_weights,
    dec_weights,
    enc_bias,
    enc_gain,
    mesh_bias,
    mesh_gain,
    dec_bias,
    dec_gain,
):
    rows, columns = mesh_latent.shape
    size = lax.axis_size("nodes")
    to_near = [(j, j ^ 1) for j in range(size)]
    onward = [(j, (j + 2 - 4 * (j % 2)) % size) for j in range(size)]
    core = lax.axis_index("feat").astype(jnp.int32).reshape(1)
    parity = (lax.axis_index("nodes") % 2).astype(jnp.int32).reshape(1)
    arrived = exchange(pick_rows(grid_order, grid_latent))

    chunks = math.gcd(CHUNKS, rows // BLOCK)
    prepared = prepare(
        rows // BLOCK,
        chunks,
        parity,
        class_gain,
        (enc_send_block, enc_recv_block, enc_live, enc_classes),
        (mesh_send_block, mesh_recv_block, mesh_live, mesh_classes),
        (dec_send_block, dec_recv_block, dec_live, dec_classes),
    )
    e_off = enc_offsets.reshape(-1, BLOCK)
    m_off = mesh_offsets.reshape(-1, BLOCK)
    d_off = dec_offsets.reshape(-1, BLOCK)
    outs = [enc_weights[2], mesh_weights[0, 2], mesh_weights[1, 2], dec_weights[2]]
    outs_other = [swap(outs[0])]
    gains = [enc_gain[None, :], mesh_gain]
    gains_other = [swap(x) for x in gains]
    xm, xt = mesh_latent, swap(mesh_latent)
    take = project(core, xm, xt, enc_weights[1], enc_bias[None, :])
    arrived, prepared, take, outs_other, gains_other = tie(
        arrived, prepared, take, outs_other, gains_other
    )
    gains = [gains[0], gains[1][:1], gains[1][1:]]
    gains_other = [gains_other[0], gains_other[1][:1], gains_other[1][1:]]
    e_list, m_list, d_list, counts, e_w, m_w, d_w = prepared
    length = list_length(mesh_send_block.shape[0])

    arrived_other = swap(arrived)
    nothing = jnp.zeros((1, columns), F32)
    send = project(core, arrived, arrived_other, enc_weights[0], nothing)
    agg = edge_sum(0, 0, counts, e_list, [send], take, e_off, e_w, None, True)
    grid_take = project(core, arrived, arrived_other, dec_weights[1], dec_bias[None, :])
    for r in range(ROUNDS):
        xm, xt, send = mix(
            core,
            agg,
            swap(agg),
            xm,
            xt,
            outs[r],
            outs_other[r],
            gains[r],
            gains_other[r],
            mesh_weights[r, 0],
        )
        near = [ring(x, to_near) for x in jnp.split(send, chunks)]
        take = project(core, xm, xt, mesh_weights[r, 1], mesh_bias[r][None, :])
        common = (take, m_off, m_w)
        total = None
        far = []
        for k in range(chunks):
            if total is None:
                near[k], take = tie(near[k], take)
                common = (take, m_off, m_w)
            else:
                near[k], total = tie(near[k], total)
            far.append(ring(near[k], onward))
            if k < own_parts(chunks):
                total = edge_sum(
                    5 + k,
                    (3 + k) * length,
                    counts,
                    m_list,
                    [send],
                    *common,
                    total,
                    False,
                )
        fresh = outs[r + 1 : r + 2] if r + 1 < ROUNDS else outs[r + 1 :]
        fresh, total = tie(fresh, total)
        fresh = [swap(w) for w in fresh]
        total = edge_sum(2, 0, counts, m_list, near, *common, total, False)
        total, fresh = tie(total, fresh)
        outs_other += fresh
        if chunks > 1:
            total = edge_sum(3, length, counts, m_list, far[:-1], *common, total, False)
        agg = edge_sum(4, 2 * length, counts, m_list, far[-1:], *common, total, True)
    xm, xt, send = mix(
        core,
        agg,
        swap(agg),
        xm,
        xt,
        outs[ROUNDS],
        outs_other[ROUNDS],
        gains[ROUNDS],
        gains_other[ROUNDS],
        dec_weights[0],
    )
    agg = edge_sum(1, 0, counts, d_list, [send], grid_take, d_off, d_w, None, True)
    update = update_of(
        core, agg, swap(agg), outs[3], outs_other[3], dec_gain[None, :]
    )
    grid_out = place_rows(grid_order, exchange(update), grid_latent)
    return grid_out, xm


def solution(mesh):
    in_specs = (
        P("nodes", "feat"),
        P("nodes", "feat"),
        P("nodes", None),
        P("nodes"),
        P("nodes"),
        P("nodes", None, None),
        P("nodes", None),
        P("nodes"),
        P("nodes"),
        P("nodes"),
        P("nodes", None, None),
        P("nodes", None),
        P("nodes"),
        P("nodes"),
        P("nodes"),
        P("nodes", None, None),
        P("nodes", None),
        P("nodes"),
        P(),
        P(None, None, "feat"),
        P(None, None, None, "feat"),
        P(None, None, "feat"),
        P("feat"),
        P("feat"),
        P(None, "feat"),
        P(None, "feat"),
        P("feat"),
        P("feat"),
    )
    out_specs = (P("nodes", "feat"), P("nodes", "feat"))
    return jax.shard_map(
        local, mesh=mesh, in_specs=in_specs, out_specs=out_specs, check_vma=False
    )
```

profile of v0, /device:TPU:0, one launch (start us, length us, event | category | flops | bytes accessed | tf_op | source)
XLA Modules:
  0.0 145.5 jit_solution(1502652412071191055)
XLA Ops:
  0.6 2.7 %shard_map.275 = bf16[1024,256]{1,0:T(8,128)(2,1)} custom-call(s32[1,1024]{1,0:T(1,128)} %order.1, bf16[1024,256]{1,0:T(8,128)(2,1)} %rest.1), custom_call_target="tpu_custom_call" | custom-call | tf_op jit(solution)/shard_map/pallas_call | solution.py:375
  3.5 8.5 %all-to-all-start = ((bf16[16,64,256]{2,1,0:T(8,128)(2,1)}), bf16[16,64,256]{2,1,0:T(8,128)(2,1)S(1)}, u32[]{:S(2)}, u32[]{:S(2)}) async-start(bf16[16,64,256]{2,1,0:T(8,128)(2,1)} %bitcast.61), calls=%async_computation | async-start | bytes 1048576 | tf_op jit(solution)/shard_map/all_to_all | solution.py:416
  16.4 4.7 %shard_map.276 = (s32[24]{0:T(128)S(1)}, s32[624]{0:T(1024)S(1)}, s32[32]{0:T(128)S(1)}, s32[12]{0:T(128)S(1)}, f32[16,128]{1,0:T(8,128)S(1)}, /*index=5*/f32[96,128]{1,0:T(8,128)S(1)}, f32[24,128]{1,0:T(8,128)S(1)}) custom-call(s32[1]{0:T(128)} %bitcast.3.parity, f32[3,8]{1,0:T(4,128)S(1)} %copy-done.15, s32[16]{0:T(128)S(1)} %copy-done.16, ...), custom_call_target="tpu_custom_call" | custom-call | flops 2000000000 | bytes 1000000 | tf_op jit(solution)/shard_map/pallas_call | solution.py:136
  22.3 4.8 %all-to-all-done = bf16[16,64,256]{2,1,0:T(8,128)(2,1)S(1)} async-done(((bf16[16,64,256]{2,1,0:T(8,128)(2,1)}), bf16[16,64,256]{2,1,0:T(8,128)(2,1)S(1)}, u32[]{:S(2)}, u32[]{:S(2)}) %all-to-all-start) | async-done | bytes 524320 | tf_op jit(solution)/shard_map/all_to_all | solution.py:416
  29.4 2.1 %shard_map.279.am = bf16[1024,256]{1,0:T(8,128)(2,1)S(1)} custom-call(s32[12]{0:T(128)S(1)} %get-tuple-element.62.counts, s32[24]{0:T(128)S(1)} %get-tuple-element.65.items, bf16[1024,256]{1,0:T(8,128)(2,1)S(1)} %shard_map.278.refs_0_, bf16[1024,256]{1,0:T(8,128)(2,1)S(1)} %shard_map.277.refs_1_, s32[32,128]{1,0:T(8,128)S(1)} %bitcast.60, ...), custom_call_target="tpu_custom_call" | custom-call | flops 2000000000 | bytes 2000000 | tf_op jit(solution)/shard_map/pallas_call | solution.py:246
  42.1 2.1 %shard_map.282.refs_4_ = f32[1152,256]{1,0:T(8,128)S(1)} custom-call(s32[12]{0:T(128)S(1)} %get-tuple-element.62.counts, s32[624]{0:T(1024)S(1)} %get-tuple-element.64.items, bf16[1024,256]{1,0:T(8,128)(2,1)S(1)} %get-tuple-element.71.refs_0_, bf16[1024,256]{1,0:T(8,128)(2,1)S(1)} %shard_map.281.refs_1_.refs_4_.refs_3_, s32[192,128]{1,0:T(8,128)S(1)} %bitcast.47, ...), custom_call_target="tpu_custom_call" | custom-call | flops 2000000000 | bytes 2000000 | tf_op jit(solution)/shard_map/pallas_call | solution.py:246
  44.1 5.5 %collective-permute-done.9.refs_1_ = bf16[256,256]{1,0:T(8,128)(2,1)S(1)} collective-permute-done((bf16[256,256]{1,0:T(8,128)(2,1)S(1)}, bf16[256,256]{1,0:T(8,128)(2,1)S(1)}, u32[]{:S(2)}, u32[]{:S(2)}) %collective-permute-start.9) | collective-permute-done | bytes 131104 | tf_op jit(solution)/shard_map/ppermute | solution.py:424
  49.6 2.0 %shard_map.283.refs_4_ = f32[1152,256]{1,0:T(8,128)S(1)} custom-call(s32[12]{0:T(128)S(1)} %get-tuple-element.62.counts, s32[624]{0:T(1024)S(1)} %get-tuple-element.64.items, bf16[1024,256]{1,0:T(8,128)(2,1)S(1)} %get-tuple-element.71.refs_0_, bf16[1024,256]{1,0:T(8,128)(2,1)S(1)} %shard_map.281.refs_1_.refs_4_.refs_3_, ...), custom_call_target="tpu_custom_call", output_to_operand_aliasing={{}: (6, {})} | custom-call | flops 2000000000 | bytes 2000000 | tf_op jit(solution)/shard_map/pallas_call | solution.py:246
  56.9 3.6 %shard_map.285.refs_6_ = f32[1152,256]{1,0:T(8,128)S(1)} custom-call(s32[12]{0:T(128)S(1)} %get-tuple-element.62.counts, s32[624]{0:T(1024)S(1)} %get-tuple-element.64.items, bf16[256,256]{1,0:T(8,128)(2,1)S(1)} %collective-permute-done.7.refs_0_, bf16[256,256]{1,0:T(8,128)(2,1)S(1)} %collective-permute-done.9.refs_1_, ...), custom_call_target="tpu_custom_call", output_to_operand_aliasing={{}: (9, {})} | custom-call | flops 2000000000 | bytes 2000000 | tf_op jit(solution)/shard_map/pallas_call | solution.py:246
  60.5 4.9 %collective-permute-done.11.refs_0_ = bf16[256,256]{1,0:T(8,128)(2,1)S(1)} collective-permute-done((bf16[256,256]{1,0:T(8,128)(2,1)S(1)}, bf16[256,256]{1,0:T(8,128)(2,1)S(1)}, u32[]{:S(2)}, u32[]{:S(2)}) %collective-permute-start.11) | collective-permute-done | bytes 131104 | tf_op jit(solution)/shard_map/ppermute | solution.py:424
  65.4 2.8 %collective-permute-done.12.refs_1_ = bf16[256,256]{1,0:T(8,128)(2,1)S(1)} collective-permute-done((bf16[256,256]{1,0:T(8,128)(2,1)S(1)}, bf16[256,256]{1,0:T(8,128)(2,1)S(1)}, u32[]{:S(2)}, u32[]{:S(2)}) %collective-permute-start.12) | collective-permute-done | bytes 131104 | tf_op jit(solution)/shard_map/ppermute | solution.py:424
  68.2 2.3 %collective-permute-done.13.refs_2_ = bf16[256,256]{1,0:T(8,128)(2,1)S(1)} collective-permute-done((bf16[256,256]{1,0:T(8,128)(2,1)S(1)}, bf16[256,256]{1,0:T(8,128)(2,1)S(1)}, u32[]{:S(2)}, u32[]{:S(2)}) %collective-permute-start.13) | collective-permute-done | bytes 131104 | tf_op jit(solution)/shard_map/ppermute | solution.py:424
  70.5 2.4 %shard_map.286.refs_4_ = f32[1152,256]{1,0:T(8,128)S(1)} custom-call(s32[12]{0:T(128)S(1)} %get-tuple-element.62.counts, s32[624]{0:T(1024)S(1)} %get-tuple-element.64.items, bf16[256,256]{1,0:T(8,128)(2,1)S(1)} %collective-permute-done.11.refs_0_, bf16[256,256]{1,0:T(8,128)(2,1)S(1)} %collective-permute-done.12.refs_1_, ...), custom_call_target="tpu_custom_call", output_to_operand_aliasing={{}: (8, {})} | custom-call | flops 2000000000 | bytes 2000000 | tf_op jit(solution)/shard_map/pallas_call | solution.py:246
  85.1 2.1 %shard_map.290.refs_4_ = f32[1152,256]{1,0:T(8,128)S(1)} custom-call(s32[12]{0:T(128)S(1)} %get-tuple-element.62.counts, s32[624]{0:T(1024)S(1)} %get-tuple-element.64.items, bf16[1024,256]{1,0:T(8,128)(2,1)S(1)} %get-tuple-element.88.refs_0_, bf16[1024,256]{1,0:T(8,128)(2,1)S(1)} %shard_map.289.refs_1_.refs_4_.refs_3_, s32[192,128]{1,0:T(8,128)S(1)} %bitcast.53, ...), custom_call_target="tpu_custom_call" | custom-call | flops 2000000000 | bytes 2000000 | tf_op jit(solution)/shard_map/pallas_call | solution.py:246
  87.1 5.5 %collective-permute-done.19.refs_1_ = bf16[256,256]{1,0:T(8,128)(2,1)S(1)} collective-permute-done((bf16[256,256]{1,0:T(8,128)(2,1)S(1)}, bf16[256,256]{1,0:T(8,128)(2,1)S(1)}, u32[]{:S(2)}, u32[]{:S(2)}) %collective-permute-start.19) | collective-permute-done | bytes 131104 | tf_op jit(solution)/shard_map/ppermute | solution.py:424
  92.7 2.0 %shard_map.291.refs_4_ = f32[1152,256]{1,0:T(8,128)S(1)} custom-call(s32[12]{0:T(128)S(1)} %get-tuple-element.62.counts, s32[624]{0:T(1024)S(1)} %get-tuple-element.64.items, bf16[1024,256]{1,0:T(8,128)(2,1)S(1)} %get-tuple-element.88.refs_0_, bf16[1024,256]{1,0:T(8,128)(2,1)S(1)} %shard_map.289.refs_1_.refs_4_.refs_3_, ...), custom_call_target="tpu_custom_call", output_to_operand_aliasing={{}: (6, {})} | custom-call | flops 2000000000 | bytes 2000000 | tf_op jit(solution)/shard_map/pallas_call | solution.py:246
  97.0 3.6 %shard_map.293.refs_6_ = f32[1152,256]{1,0:T(8,128)S(1)} custom-call(s32[12]{0:T(128)S(1)} %get-tuple-element.62.counts, s32[624]{0:T(1024)S(1)} %get-tuple-element.64.items, bf16[256,256]{1,0:T(8,128)(2,1)S(1)} %collective-permute-done.17.refs_0_, bf16[256,256]{1,0:T(8,128)(2,1)S(1)} %collective-permute-done.19.refs_1_, ...), custom_call_target="tpu_custom_call", output_to_operand_aliasing={{}: (9, {})} | custom-call | flops 2000000000 | bytes 2000000 | tf_op jit(solution)/shard_map/pallas_call | solution.py:246
  100.7 5.3 %collective-permute-done.21.refs_0_ = bf16[256,256]{1,0:T(8,128)(2,1)S(1)} collective-permute-done((bf16[256,256]{1,0:T(8,128)(2,1)S(1)}, bf16[256,256]{1,0:T(8,128)(2,1)S(1)}, u32[]{:S(2)}, u32[]{:S(2)}) %collective-permute-start.21) | collective-permute-done | bytes 131104 | tf_op jit(solution)/shard_map/ppermute | solution.py:424
  106.1 2.8 %collective-permute-done.22.refs_1_ = bf16[256,256]{1,0:T(8,128)(2,1)S(1)} collective-permute-done((bf16[256,256]{1,0:T(8,128)(2,1)S(1)}, bf16[256,256]{1,0:T(8,128)(2,1)S(1)}, u32[]{:S(2)}, u32[]{:S(2)}) %collective-permute-start.22) | collective-permute-done | bytes 131104 | tf_op jit(solution)/shard_map/ppermute | solution.py:424
  108.9 2.8 %collective-permute-done.23.refs_2_ = bf16[256,256]{1,0:T(8,128)(2,1)S(1)} collective-permute-done((bf16[256,256]{1,0:T(8,128)(2,1)S(1)}, bf16[256,256]{1,0:T(8,128)(2,1)S(1)}, u32[]{:S(2)}, u32[]{:S(2)}) %collective-permute-start.23) | collective-permute-done | bytes 131104 | tf_op jit(solution)/shard_map/ppermute | solution.py:424
  111.7 2.4 %shard_map.294.refs_4_ = f32[1152,256]{1,0:T(8,128)S(1)} custom-call(s32[12]{0:T(128)S(1)} %get-tuple-element.62.counts, s32[624]{0:T(1024)S(1)} %get-tuple-element.64.items, bf16[256,256]{1,0:T(8,128)(2,1)S(1)} %collective-permute-done.21.refs_0_, bf16[256,256]{1,0:T(8,128)(2,1)S(1)} %collective-permute-done.22.refs_1_, ...), custom_call_target="tpu_custom_call", output_to_operand_aliasing={{}: (8, {})} | custom-call | flops 2000000000 | bytes 2000000 | tf_op jit(solution)/shard_map/pallas_call | solution.py:246
  117.6 2.8 %shard_map.296 = (bf16[1024,256]{1,0:T(8,128)(2,1)}, bf16[1024,256]{1,0:T(8,128)(2,1)}, bf16[1024,256]{1,0:T(8,128)(2,1)S(1)}) custom-call(s32[1]{0:T(128)} %bitcast.core, bf16[1024,256]{1,0:T(8,128)(2,1)S(1)} %shard_map.295.am, bf16[1024,256]{1,0:T(8,128)(2,1)S(1)} %collective-permute-done.26.at, bf16[1024,256]{1,0:T(8,128)(2,1)S(1)} %get-tuple-element.89.xm, ...), custom_call_target="tpu_custom_call" | custom-call | tf_op jit(solution)/shard_map/pallas_call | solution.py:297
  120.4 2.7 %shard_map.298.am = bf16[1024,256]{1,0:T(8,128)(2,1)S(1)} custom-call(s32[12]{0:T(128)S(1)} %get-tuple-element.62.counts, s32[32]{0:T(128)S(1)} %get-tuple-element.63.items, bf16[1024,256]{1,0:T(8,128)(2,1)S(1)} %get-tuple-element.104.refs_0_, bf16[1024,256]{1,0:T(8,128)(2,1)S(1)} %shard_map.297.refs_1_, s32[48,128]{1,0:T(8,128)S(1)} %bitcast.59, ...), custom_call_target="tpu_custom_call" | custom-call | flops 2000000000 | bytes 2000000 | tf_op jit(solution)/shard_map/pallas_call | solution.py:246
  125.9 18.1 %all_to_all.23 = bf16[16,64,256]{2,1,0:T(8,128)(2,1)S(1)} all-to-all(bf16[16,64,256]{2,1,0:T(8,128)(2,1)S(1)} %bitcast.41), channel_id=1, replica_groups=mesh['nodes'=16,'feat'=2] {'nodes'}, dimensions={0} | all-to-all | bytes 1048576 | tf_op jit(solution)/shard_map/all_to_all | solution.py:416
  (122 shorter events, 43.8 us)
Async XLA Ops:
  3.5 23.6 %all-to-all-start = ((bf16[16,64,256]{2,1,0:T(8,128)(2,1)}), bf16[16,64,256]{2,1,0:T(8,128)(2,1)S(1)}, u32[]{:S(2)}, u32[]{:S(2)}) async-start(bf16[16,64,256]{2,1,0:T(8,128)(2,1)} %bitcast.61), calls=%async_computation | async-start | bytes 1048576 | tf_op jit(solution)/shard_map/all_to_all | solution.py:416
  12.0 9.1 %collective-permute-start = (bf16[1024,256]{1,0:T(8,128)(2,1)S(1)}, bf16[1024,256]{1,0:T(8,128)(2,1)S(1)}, u32[]{:S(2)}, u32[]{:S(2)}) collective-permute-start(bf16[1024,256]{1,0:T(8,128)(2,1)S(1)} %copy-done.1), channel_id=1, source_target_pairs={{0,1},{1,0},{2,3},{3,2},{4,5},{5,4},{6,7},{7,6},{8,9},{9,8},{10,11... | collective-permute-start | bytes 1572872 | tf_op jit(solution)/shard_map/ppermute | solution.py:412
  13.2 8.3 %collective-permute-start.1 = (bf16[512,256]{1,0:T(8,128)(2,1)S(1)}, bf16[512,256]{1,0:T(8,128)(2,1)S(1)}, u32[]{:S(2)}, u32[]{:S(2)}) collective-permute-start(bf16[512,256]{1,0:T(8,128)(2,1)S(1)} %get-tuple-element.119.wm), channel_id=1, source_target_pairs={{0,1},{1,0},{2,3},{3,2},{4,5},{5,4},{6,7},{7,6},{8,9},{9,8},{10,11... | collective-permute-start | bytes 786440 | tf_op jit(solution)/shard_map/ppermute | solution.py:412
  13.8 7.8 %collective-permute-start.2 = (f32[1,256]{1,0:T(1,128)S(1)}, f32[1,256]{1,0:T(1,128)S(1)}, u32[]{:S(2)}, u32[]{:S(2)}) collective-permute-start(f32[1,256]{1,0:T(1,128)S(1)} %bitcast.43), channel_id=1, source_target_pairs={{0,1},{1,0},{2,3},{3,2},{4,5},{5,4},{6,7},{7,6},{8,9},{9,8},{10,11... | collective-permute-start | bytes 3080 | tf_op jit(solution)/shard_map/ppermute | solution.py:412
  13.9 7.7 %collective-permute-start.3 = (f32[2,256]{1,0:T(2,128)S(1)}, f32[2,256]{1,0:T(2,128)S(1)}, u32[]{:S(2)}, u32[]{:S(2)}) collective-permute-start(f32[2,256]{1,0:T(2,128)S(1)} %copy-done.25), channel_id=1, source_target_pairs={{0,1},{1,0},{2,3},{3,2},{4,5},{5,4},{6,7},{7,6},{8,9},{9,8},{10,11... | collective-permute-start | bytes 6152 | tf_op jit(solution)/shard_map/ppermute | solution.py:412
  35.6 6.4 %collective-permute-start.7 = (bf16[256,256]{1,0:T(8,128)(2,1)S(1)}, bf16[256,256]{1,0:T(8,128)(2,1)S(1)}, u32[]{:S(2)}, u32[]{:S(2)}) collective-permute-start(bf16[256,256]{1,0:T(8,128)(2,1)S(1)} %get-tuple-element.126), channel_id=1, source_target_pairs={{0,2},{2,0},{4,6},{6,4},{8,10},{10,8},{12,14},{14,12},{16,18},{18,... | collective-permute-start | bytes 393224 | tf_op jit(solution)/shard_map/ppermute | solution.py:424
  35.9 17.5 %collective-permute-start.6 = (bf16[256,256]{1,0:T(8,128)(2,1)S(1)}, bf16[256,256]{1,0:T(8,128)(2,1)S(1)}, u32[]{:S(2)}, u32[]{:S(2)}) collective-permute-start(bf16[256,256]{1,0:T(8,128)(2,1)S(1)} %get-tuple-element.127), channel_id=1, source_target_pairs={{0,2},{2,0},{4,6},{6,4},{8,10},{10,8},{12,14},{14,12},{16,18},{18,... | collective-permute-start | bytes 393224 | tf_op jit(solution)/shard_map/ppermute | solution.py:424
  37.7 14.0 %collective-permute-start.8 = (bf16[256,256]{1,0:T(8,128)(2,1)S(1)}, bf16[256,256]{1,0:T(8,128)(2,1)S(1)}, u32[]{:S(2)}, u32[]{:S(2)}) collective-permute-start(bf16[256,256]{1,0:T(8,128)(2,1)S(1)} %get-tuple-element.125), channel_id=1, source_target_pairs={{0,2},{2,0},{4,6},{6,4},{8,10},{10,8},{12,14},{14,12},{16,18},{18,... | collective-permute-start | bytes 393224 | tf_op jit(solution)/shard_map/ppermute | solution.py:424
  38.0 11.7 %collective-permute-start.9 = (bf16[256,256]{1,0:T(8,128)(2,1)S(1)}, bf16[256,256]{1,0:T(8,128)(2,1)S(1)}, u32[]{:S(2)}, u32[]{:S(2)}) collective-permute-start(bf16[256,256]{1,0:T(8,128)(2,1)S(1)} %get-tuple-element.124), channel_id=1, source_target_pairs={{0,2},{2,0},{4,6},{6,4},{8,10},{10,8},{12,14},{14,12},{16,18},{18,... | collective-permute-start | bytes 393224 | tf_op jit(solution)/shard_map/ppermute | solution.py:424
  53.4 7.1 %collective-permute-start.14 = (bf16[512,256]{1,0:T(8,128)(2,1)S(1)}, bf16[512,256]{1,0:T(8,128)(2,1)S(1)}, u32[]{:S(2)}, u32[]{:S(2)}) collective-permute-start(bf16[512,256]{1,0:T(8,128)(2,1)S(1)} %get-tuple-element.84.wm), channel_id=1, source_target_pairs={{0,1},{1,0},{2,3},{3,2},{4,5},{5,4},{6,7},{7,6},{8,9},{9,8},{10,11... | collective-permute-start | bytes 786440 | tf_op jit(solution)/shard_map/ppermute | solution.py:412
  53.5 19.4 %collective-permute-start.10 = (bf16[256,256]{1,0:T(8,128)(2,1)S(1)}, bf16[256,256]{1,0:T(8,128)(2,1)S(1)}, u32[]{:S(2)}, u32[]{:S(2)}) collective-permute-start(bf16[256,256]{1,0:T(8,128)(2,1)S(1)} %collective-permute-done.6.refs_3_), channel_id=1, source_target_pairs={{0,4},{2,30},{4,8},{6,2},{8,12},{10,6},{12,16},{14,10},{16,20},{18... | collective-permute-start | bytes 393224 | tf_op jit(solution)/shard_map/ppermute | solution.py:424
  53.6 11.9 %collective-permute-start.11 = (bf16[256,256]{1,0:T(8,128)(2,1)S(1)}, bf16[256,256]{1,0:T(8,128)(2,1)S(1)}, u32[]{:S(2)}, u32[]{:S(2)}) collective-permute-start(bf16[256,256]{1,0:T(8,128)(2,1)S(1)} %collective-permute-done.7.refs_0_), channel_id=1, source_target_pairs={{0,4},{2,30},{4,8},{6,2},{8,12},{10,6},{12,16},{14,10},{16,20},{18... | collective-permute-start | bytes 393224 | tf_op jit(solution)/shard_map/ppermute | solution.py:424
  55.1 13.1 %collective-permute-start.12 = (bf16[256,256]{1,0:T(8,128)(2,1)S(1)}, bf16[256,256]{1,0:T(8,128)(2,1)S(1)}, u32[]{:S(2)}, u32[]{:S(2)}) collective-permute-start(bf16[256,256]{1,0:T(8,128)(2,1)S(1)} %collective-permute-done.9.refs_1_), channel_id=1, source_target_pairs={{0,4},{2,30},{4,8},{6,2},{8,12},{10,6},{12,16},{14,10},{16,20},{18... | collective-permute-start | bytes 393224 | tf_op jit(solution)/shard_map/ppermute | solution.py:424
  56.0 14.5 %collective-permute-start.13 = (bf16[256,256]{1,0:T(8,128)(2,1)S(1)}, bf16[256,256]{1,0:T(8,128)(2,1)S(1)}, u32[]{:S(2)}, u32[]{:S(2)}) collective-permute-start(bf16[256,256]{1,0:T(8,128)(2,1)S(1)} %collective-permute-done.8.refs_2_), channel_id=1, source_target_pairs={{0,4},{2,30},{4,8},{6,2},{8,12},{10,6},{12,16},{14,10},{16,20},{18... | collective-permute-start | bytes 393224 | tf_op jit(solution)/shard_map/ppermute | solution.py:424
  78.6 6.4 %collective-permute-start.17 = (bf16[256,256]{1,0:T(8,128)(2,1)S(1)}, bf16[256,256]{1,0:T(8,128)(2,1)S(1)}, u32[]{:S(2)}, u32[]{:S(2)}) collective-permute-start(bf16[256,256]{1,0:T(8,128)(2,1)S(1)} %get-tuple-element.122), channel_id=1, source_target_pairs={{0,2},{2,0},{4,6},{6,4},{8,10},{10,8},{12,14},{14,12},{16,18},{18,... | collective-permute-start | bytes 393224 | tf_op jit(solution)/shard_map/ppermute | solution.py:424
  79.8 16.7 %collective-permute-start.16 = (bf16[256,256]{1,0:T(8,128)(2,1)S(1)}, bf16[256,256]{1,0:T(8,128)(2,1)S(1)}, u32[]{:S(2)}, u32[]{:S(2)}) collective-permute-start(bf16[256,256]{1,0:T(8,128)(2,1)S(1)} %get-tuple-element.123), channel_id=1, source_target_pairs={{0,2},{2,0},{4,6},{6,4},{8,10},{10,8},{12,14},{14,12},{16,18},{18,... | collective-permute-start | bytes 393224 | tf_op jit(solution)/shard_map/ppermute | solution.py:424
  80.8 13.9 %collective-permute-start.18 = (bf16[256,256]{1,0:T(8,128)(2,1)S(1)}, bf16[256,256]{1,0:T(8,128)(2,1)S(1)}, u32[]{:S(2)}, u32[]{:S(2)}) collective-permute-start(bf16[256,256]{1,0:T(8,128)(2,1)S(1)} %get-tuple-element.121), channel_id=1, source_target_pairs={{0,2},{2,0},{4,6},{6,4},{8,10},{10,8},{12,14},{14,12},{16,18},{18,... | collective-permute-start | bytes 393224 | tf_op jit(solution)/shard_map/ppermute | solution.py:424
  81.8 10.8 %collective-permute-start.19 = (bf16[256,256]{1,0:T(8,128)(2,1)S(1)}, bf16[256,256]{1,0:T(8,128)(2,1)S(1)}, u32[]{:S(2)}, u32[]{:S(2)}) collective-permute-start(bf16[256,256]{1,0:T(8,128)(2,1)S(1)} %get-tuple-element.120), channel_id=1, source_target_pairs={{0,2},{2,0},{4,6},{6,4},{8,10},{10,8},{12,14},{14,12},{16,18},{18,... | collective-permute-start | bytes 393224 | tf_op jit(solution)/shard_map/ppermute | solution.py:424
  96.4 4.2 %collective-permute-start.24 = (bf16[512,256]{1,0:T(8,128)(2,1)S(1)}, bf16[512,256]{1,0:T(8,128)(2,1)S(1)}, u32[]{:S(2)}, u32[]{:S(2)}) collective-permute-start(bf16[512,256]{1,0:T(8,128)(2,1)S(1)} %get-tuple-element.100.wm), channel_id=1, source_target_pairs={{0,1},{1,0},{2,3},{3,2},{4,5},{5,4},{6,7},{7,6},{8,9},{9,8},{10,11... | collective-permute-start | bytes 786440 | tf_op jit(solution)/shard_map/ppermute | solution.py:412
  96.5 4.2 %collective-permute-start.25 = (bf16[512,256]{1,0:T(8,128)(2,1)S(1)}, bf16[512,256]{1,0:T(8,128)(2,1)S(1)}, u32[]{:S(2)}, u32[]{:S(2)}) collective-permute-start(bf16[512,256]{1,0:T(8,128)(2,1)S(1)} %get-tuple-element.101.wm), channel_id=1, source_target_pairs={{0,1},{1,0},{2,3},{3,2},{4,5},{5,4},{6,7},{7,6},{8,9},{9,8},{10,11... | collective-permute-start | bytes 786440 | tf_op jit(solution)/shard_map/ppermute | solution.py:412
  97.0 9.1 %collective-permute-start.21 = (bf16[256,256]{1,0:T(8,128)(2,1)S(1)}, bf16[256,256]{1,0:T(8,128)(2,1)S(1)}, u32[]{:S(2)}, u32[]{:S(2)}) collective-permute-start(bf16[256,256]{1,0:T(8,128)(2,1)S(1)} %collective-permute-done.17.refs_0_), channel_id=1, source_target_pairs={{0,4},{2,30},{4,8},{6,2},{8,12},{10,6},{12,16},{14,10},{16,20},{18... | collective-permute-start | bytes 393224 | tf_op jit(solution)/shard_map/ppermute | solution.py:424
  97.0 11.9 %collective-permute-start.22 = (bf16[256,256]{1,0:T(8,128)(2,1)S(1)}, bf16[256,256]{1,0:T(8,128)(2,1)S(1)}, u32[]{:S(2)}, u32[]{:S(2)}) collective-permute-start(bf16[256,256]{1,0:T(8,128)(2,1)S(1)} %collective-permute-done.19.refs_1_), channel_id=1, source_target_pairs={{0,4},{2,30},{4,8},{6,2},{8,12},{10,6},{12,16},{14,10},{16,20},{18... | collective-permute-start | bytes 393224 | tf_op jit(solution)/shard_map/ppermute | solution.py:424
  97.0 14.7 %collective-permute-start.23 = (bf16[256,256]{1,0:T(8,128)(2,1)S(1)}, bf16[256,256]{1,0:T(8,128)(2,1)S(1)}, u32[]{:S(2)}, u32[]{:S(2)}) collective-permute-start(bf16[256,256]{1,0:T(8,128)(2,1)S(1)} %collective-permute-done.18.refs_2_), channel_id=1, source_target_pairs={{0,4},{2,30},{4,8},{6,2},{8,12},{10,6},{12,16},{14,10},{16,20},{18... | collective-permute-start | bytes 393224 | tf_op jit(solution)/shard_map/ppermute | solution.py:424
  100.7 13.4 %collective-permute-start.20 = (bf16[256,256]{1,0:T(8,128)(2,1)S(1)}, bf16[256,256]{1,0:T(8,128)(2,1)S(1)}, u32[]{:S(2)}, u32[]{:S(2)}) collective-permute-start(bf16[256,256]{1,0:T(8,128)(2,1)S(1)} %collective-permute-done.16.refs_3_), channel_id=1, source_target_pairs={{0,4},{2,30},{4,8},{6,2},{8,12},{10,6},{12,16},{14,10},{16,20},{18... | collective-permute-start | bytes 393224 | tf_op jit(solution)/shard_map/ppermute | solution.py:424
  (31 other events, 245.6 us)
where the time goes:
time: 146 us
  Pallas kernels  50.3 us (34%)
  waiting for transfers between devices  49 us (34%)
  starting transfers between devices  21.5 us (15%)
  blocking collectives  18.1 us (12%)
  between operations  3.29 us (2%)
  local copies, waits for them, and re-layouts  3.24 us (2%)
    ppermute x16, waiting for transfers between devices, ring(): return lax.ppermute(chunk, 'nodes', pairs)  35.6 us
    pallas_call x14, Pallas kernels, edge_sum(): pl.pallas_call(functools.partial(edge_kernel, where, base, len(sends), fi...  31.6 us
    all_to_all x1, blocking collectives, exchange(): return lax.all_to_all(x, 'nodes', split_axis=0, concat_axis=0, tiled=True)  18.1 us
    ppermute x16, starting transfers between devices, ring(): return lax.ppermute(chunk, 'nodes', pairs)  10.7 us
    ppermute x12, waiting for transfers between devices, swap(): return lax.ppermute(x, 'feat', [(0, 1), (1, 0)])  8.67 us
    all_to_all x1, starting transfers between devices, exchange(): return lax.all_to_all(x, 'nodes', split_axis=0, concat_axis=0, tiled=True)  8.48 us
    pallas_call x3, Pallas kernels, mix(): pl.pallas_call(mix_kernel, out_shape=[shape] * 3, in_specs=[SMEM] + [VMEM...  6.79 us
    all_to_all x1, waiting for transfers between devices, exchange(): return lax.all_to_all(x, 'nodes', split_axis=0, concat_axis=0, tiled=True)  4.78 us
  transfers between devices with their start and end apart: 29, of which 16 were waited for; matrix products, arithmetic and copies ran while one was open for 1% of the time, Pallas kernels for 21%

commit v1 on v0

--- a/solution.py
+++ b/solution.py
@@ -13,6 +13,7 @@
 ROUNDS = 2
 UNROLL = 4
 CHUNKS = 4
+HALVES = 2
 EPSILON = 1e-05
 
 VMEM = pl.BlockSpec(memory_space=pltpu.VMEM)
@@ -196,16 +197,19 @@
     scatter(trips - 1)
 
 
-def edge_kernel(where, base, pieces_in, first, last, counts, items, *refs):
+def edge_kernel(where, base, pieces_in, halves, first, counts, items, *refs):
+    last = halves > 0
     refs = list(refs)
     sends = [refs.pop(0) for _ in range(pieces_in)]
     take, offsets, weights = refs[:3]
     refs = refs[3:]
     if not first:
         before = refs.pop(0)
-    out, picks, held = refs[:3]
-    refs = refs[3:]
-    acc = refs.pop(0) if last else out
+    outs = refs[: max(halves, 1)]
+    refs = refs[max(halves, 1) :]
+    picks, held = refs[:2]
+    refs = refs[2:]
+    acc = refs.pop(0) if last else outs[0]
     if first:
         acc[...] = jnp.zeros_like(acc)
     elif last:
@@ -218,11 +222,13 @@
             joined[pl.ds(k * depth, depth), :] = piece[...]
         send = joined
     edge_loop(base, counts[where], items, send, take, offsets, weights, acc, picks, held)
-    if last:
-        out[...] = acc[pl.ds(0, out.shape[0]), :].astype(out.dtype)
-
-
-def edge_sum(where, base, counts, items, sends, take, offsets, weights, before, last):
+    for k, out in enumerate(outs[:halves]):
+        depth = out.shape[0]
+        out[...] = acc[pl.ds(k * depth, depth), :].astype(out.dtype)
+
+
+def edge_sum(where, base, counts, items, sends, take, offsets, weights, before, halves):
+    last = halves > 0
     first = before is None
     rows, columns = take.shape
     arrays = [counts, items, *sends, take, offsets, weights]
@@ -237,17 +243,17 @@
     ]
     if last:
         scratch.append(pltpu.VMEM(full, F32))
-        shape = jax.ShapeDtypeStruct((rows, columns), BF16)
+        shape = [jax.ShapeDtypeStruct((rows // halves, columns), BF16)] * halves
     else:
-        shape = jax.ShapeDtypeStruct(full, F32)
+        shape = [jax.ShapeDtypeStruct(full, F32)]
     if len(sends) > 1:
         depth = sum(x.shape[0] for x in sends)
         scratch.append(pltpu.VMEM((depth, columns), BF16))
-    return pl.pallas_call(
-        functools.partial(edge_kernel, where, base, len(sends), first, last),
+    result = pl.pallas_call(
+        functools.partial(edge_kernel, where, base, len(sends), halves, first),
         out_shape=shape,
         in_specs=[SMEM, SMEM] + [VMEM] * (len(arrays) - 2),
-        out_specs=VMEM,
+        out_specs=[VMEM] * len(shape),
         scratch_shapes=scratch,
         input_output_aliases=aliases,
         compiler_params=params(),
@@ -255,6 +261,7 @@
             flops=2_000_000_000, bytes_accessed=2_000_000, transcendentals=1_000_000
         ),
     )(*arrays)
+    return list(result) if last else result[0]
 
 
 def two_dots(a, b, weights, mine, other, width):
@@ -271,10 +278,11 @@
 
 
 def mix_kernel(
-    core, am, at, xm, xt, wm, wt, gm, gt, ws, out_m, out_t, out_s
+    chunks, core, am, at, xm, xt, wm, wt, gm, gt, ws, out_m, *outs
 ):
     rows, width = am.shape
-    tile = pieces(rows)
+    out_s, out_t = outs[:chunks], outs[chunks:]
+    tile = rows // chunks
     mine = pl.multiple_of(core[0] * width, width)
     other = pl.multiple_of(width - core[0] * width, width)
 
@@ -288,41 +296,81 @@
         nm = (xm[part, :].astype(F32) + (ym - mean) * scale * gm[...]).astype(BF16)
         nt = (xt[part, :].astype(F32) + (yt - mean) * scale * gt[...]).astype(BF16)
         out_m[part, :] = nm
-        out_t[part, :] = nt
-        out_s[part, :] = (0.5 * two_dots(nm, nt, ws, mine, other, width)).astype(BF16)
-
-
-def mix(core, am, at, xm, xt, wm, wt, gm, gt, ws):
-    shape = jax.ShapeDtypeStruct(am.shape, BF16)
-    return pl.pallas_call(
-        mix_kernel,
-        out_shape=[shape] * 3,
+        for out in out_t:
+            out[part, :] = nt
+        out_s[t][...] = (0.5 * two_dots(nm, nt, ws, mine, other, width)).astype(BF16)
+
+
+def mix(chunks, last, core, am, at, xm, xt, wm, wt, gm, gt, ws):
+    rows, width = am.shape
+    shapes = [jax.ShapeDtypeStruct((rows, width), BF16)]
+    shapes += [jax.ShapeDtypeStruct((rows // chunks, width), BF16)] * chunks
+    shapes += shapes[:1] * (not last)
+    new_xm, *rest = pl.pallas_call(
+        functools.partial(mix_kernel, chunks),
+        out_shape=shapes,
         in_specs=[SMEM] + [VMEM] * 9,
-        out_specs=[VMEM] * 3,
+        out_specs=[VMEM] * len(shapes),
         compiler_params=params(),
     )(core, am, at, xm, xt, wm, wt, gm, gt, ws)
-
-
-def project_kernel(core, xm, xt, w, bias, out):
-    rows, width = xm.shape
-    tile = pieces(rows)
+    return new_xm, rest[:chunks], rest[chunks:]
+
+
+def mix_halves(chunks, last, core, aggs, xms, xts, *rest):
+    others = [swap(x) for x in aggs]
+    results = [
+        mix(chunks // len(aggs), last, core, am, at, xm, xt, *rest)
+        for am, at, xm, xt in zip(aggs, others, xms, xts)
+    ]
+    send = [x for _, part, _ in results for x in part]
+    return [x for x, _, _ in results], [x for _, _, t in results for x in t], send
+
+
+def copy_kernel(*refs):
+    ins, out = refs[:-1], refs[-1]
+    depth = ins[0].shape[0]
+    for k, x in enumerate(ins):
+        out[pl.ds(k * depth, depth), :] = x[...]
+
+
+def joined_rows(xs):
+    rows, width = xs[0].shape
+    return pl.pallas_call(
+        copy_kernel,
+        out_shape=jax.ShapeDtypeStruct((rows * len(xs), width), BF16),
+        in_specs=[VMEM] * len(xs),
+        out_specs=VMEM,
+        compiler_params=params(4),
+    )(*xs)
+
+
+def project_kernel(core, *refs):
+    w, bias, out = refs[-3:]
+    parts = len(refs[:-3]) // 2
+    depth, width = refs[0].shape
+    rows = depth * parts
+    tile = pieces(depth)
     mine = pl.multiple_of(core[0] * width, width)
     other = pl.multiple_of(width - core[0] * width, width)
 
     for t in range(rows // tile):
         part = pl.ds(t * tile, tile)
-        y = two_dots(xm[part, :], xt[part, :], w, mine, other, width)
+        which, inner = divmod(t * tile, depth)
+        inner = pl.ds(inner, tile)
+        xm, xt = refs[which], refs[parts + which]
+        y = two_dots(xm[inner, :], xt[inner, :], w, mine, other, width)
         out[part, :] = (0.5 * (y + bias[...])).astype(BF16)
 
 
 def project(core, xm, xt, w, bias):
+    rows, width = xm[0].shape
     return pl.pallas_call(
         project_kernel,
-        out_shape=jax.ShapeDtypeStruct(xm.shape, BF16),
-        in_specs=[SMEM] + [VMEM] * 4,
+        out_shape=jax.ShapeDtypeStruct((rows * len(xm), width), BF16),
+        in_specs=[SMEM] + [VMEM] * (2 * len(xm) + 2),
         out_specs=VMEM,
         compiler_params=params(),
-    )(core, xm, xt, w, bias)
+    )(core, *xm, *xt, w, bias)
 
 
 def update_kernel(core, am, at, wm, wt, gm, out):
@@ -479,10 +527,12 @@
     outs_other = [swap(outs[0])]
     gains = [enc_gain[None, :], mesh_gain]
     gains_other = [swap(x) for x in gains]
-    xm, xt = mesh_latent, swap(mesh_latent)
+    halves = math.gcd(HALVES, chunks)
+    xm = jnp.split(mesh_latent, halves)
+    xt = jnp.split(swap(mesh_latent), halves)
     take = project(core, xm, xt, enc_weights[1], enc_bias[None, :])
-    arrived, prepared, take, outs_other, gains_other = tie(
-        arrived, prepared, take, outs_other, gains_other
+    arrived, prepared, take, outs_other, gains_other, xm, xt = tie(
+        arrived, prepared, take, outs_other, gains_other, xm, xt
     )
     gains = [gains[0], gains[1][:1], gains[1][1:]]
     gains_other = [gains_other[0], gains_other[1][:1], gains_other[1][1:]]
@@ -491,14 +541,15 @@
 
     arrived_other = swap(arrived)
     nothing = jnp.zeros((1, columns), F32)
-    send = project(core, arrived, arrived_other, enc_weights[0], nothing)
-    agg = edge_sum(0, 0, counts, e_list, [send], take, e_off, e_w, None, True)
-    grid_take = project(core, arrived, arrived_other, dec_weights[1], dec_bias[None, :])
+    send = project(core, [arrived], [arrived_other], enc_weights[0], nothing)
+    agg = edge_sum(0, 0, counts, e_list, [send], take, e_off, e_w, None, halves)
+    grid_take = project(core, [arrived], [arrived_other], dec_weights[1], dec_bias[None, :])
     for r in range(ROUNDS):
-        xm, xt, send = mix(
+        xm, xt, send = mix_halves(
+            chunks,
+            False,
             core,
             agg,
-            swap(agg),
             xm,
             xt,
             outs[r],
@@ -507,7 +558,7 @@
             gains_other[r],
             mesh_weights[r, 0],
         )
-        near = [ring(x, to_near) for x in jnp.split(send, chunks)]
+        near = [ring(x, to_near) for x in send]
         take = project(core, xm, xt, mesh_weights[r, 1], mesh_bias[r][None, :])
         common = (take, m_off, m_w)
         total = None
@@ -525,24 +576,26 @@
                     (3 + k) * length,
                     counts,
                     m_list,
-                    [send],
+                    send,
                     *common,
                     total,
-                    False,
+                    0,
                 )
-        fresh = outs[r + 1 : r + 2] if r + 1 < ROUNDS else outs[r + 1 :]
-        fresh, total = tie(fresh, total)
-        fresh = [swap(w) for w in fresh]
-        total = edge_sum(2, 0, counts, m_list, near, *common, total, False)
+        last_round = r + 1 == ROUNDS
+        sources = [(mesh_weights, (r, 2))] + [(dec_weights, (2,))] * last_round
+        arrays, total = tie([w for w, _ in sources], total)
+        fresh = [swap(w[index]) for w, (_, index) in zip(arrays, sources)]
+        total = edge_sum(2, 0, counts, m_list, near, *common, total, 0)
         total, fresh = tie(total, fresh)
         outs_other += fresh
         if chunks > 1:
-            total = edge_sum(3, length, counts, m_list, far[:-1], *common, total, False)
-        agg = edge_sum(4, 2 * length, counts, m_list, far[-1:], *common, total, True)
-    xm, xt, send = mix(
+            total = edge_sum(3, length, counts, m_list, far[:-1], *common, total, 0)
+        agg = edge_sum(4, 2 * length, counts, m_list, far[-1:], *common, total, halves)
+    xm, _, send = mix_halves(
+        chunks,
+        True,
         core,
         agg,
-        swap(agg),
         xm,
         xt,
         outs[ROUNDS],
@@ -551,12 +604,13 @@
         gains_other[ROUNDS],
         dec_weights[0],
     )
-    agg = edge_sum(1, 0, counts, d_list, [send], grid_take, d_off, d_w, None, True)
-    update = update_of(
-        core, agg, swap(agg), outs[3], outs_other[3], dec_gain[None, :]
-    )
-    grid_out = place_rows(grid_order, exchange(update), grid_latent)
-    return grid_out, xm
+    (agg,) = edge_sum(1, 0, counts, d_list, send, grid_take, d_off, d_w, None, 1)
+    xm, agg = tie(xm, agg)
+    other = swap(agg)
+    mesh_out = joined_rows(xm)
+    mesh_out, other = tie(mesh_out, other)
+    update = update_of(core, agg, other, outs[3], outs_other[3], dec_gain[None, :])
+    return place_rows(grid_order, exchange(update), grid_latent), mesh_out
 
 
 def solution(mesh):

time: 146 us -> 132 us (0.904)
  waiting for transfers between devices: 49 us -> 31.5 us
  starting transfers between devices: 21.5 us -> 25.5 us
    ppermute x16, waiting for transfers between devices: 35.6 us -> 21.9 us  [ring(): return lax.ppermute(chunk, 'nodes', pairs)]
    ppermute x12 -> x15, waiting for transfers between devices: 8.67 us -> 5.29 us  [swap(): return lax.ppermute(x, 'feat', [(0, 1), (1, 0)])]
    ppermute x16, starting transfers between devices: 10.7 us -> 13.4 us  [ring(): return lax.ppermute(chunk, 'nodes', pairs)]
    split x2, local copies, waits for them, and re-layouts: 0.07 us -> 2.13 us  [the longest x1 1.07 us: local(): xm = jnp.split(mesh_latent, halves)]
    unnamed x52 -> x48, local copies, waits for them, and re-layouts: 1.84 us -> 0.18 us
    ppermute x12 -> x15, starting transfers between devices: 2.32 us -> 3.72 us  [swap(): return lax.ppermute(x, 'feat', [(0, 1), (1, 0)])]
    pallas_call x22 -> x26, Pallas kernels: 40.6 us -> 41.2 us  [the longest x14 31.8 us: edge_sum(): pl.pallas_call(functools.partial(edge_kernel, where, base, len(sends), ha...]
  transfers between devices with their start and end apart: 29 -> 32, of which waited for: 16 -> 20; matrix products, arithmetic and copies ran while one was open for 1% -> 2% of each run, Pallas kernels for 21% -> 28%
where the time goes in v1:
time: 132 us
  Pallas kernels  50.9 us (39%)
  waiting for transfers between devices  31.5 us (24%)
  starting transfers between devices  25.5 us (19%)
  blocking collectives  18.1 us (14%)
  between operations  3.31 us (3%)
  local copies, waits for them, and re-layouts  2.59 us (2%)
    pallas_call x14, Pallas kernels, edge_sum(): pl.pallas_call(functools.partial(edge_kernel, where, base, len(sends), ha...  31.8 us
    ppermute x16, waiting for transfers between devices, ring(): return lax.ppermute(chunk, 'nodes', pairs)  21.9 us
    all_to_all x1, blocking collectives, exchange(): return lax.all_to_all(x, 'nodes', split_axis=0, concat_axis=0, tiled=True)  18.1 us
    ppermute x16, starting transfers between devices, ring(): return lax.ppermute(chunk, 'nodes', pairs)  13.4 us
    all_to_all x1, starting transfers between devices, exchange(): return lax.all_to_all(x, 'nodes', split_axis=0, concat_axis=0, tiled=True)  8.35 us
    pallas_call x6, Pallas kernels, mix(): pl.pallas_call(functools.partial(mix_kernel, chunks), out_shape=shapes, i...  6.37 us
    ppermute x15, waiting for transfers between devices, swap(): return lax.ppermute(x, 'feat', [(0, 1), (1, 0)])  5.29 us
    pallas_call x1, Pallas kernels, prepare(): pl.pallas_call(functools.partial(prepare_kernel, blocks, chunks), out_sha...  4.68 us
  transfers between devices with their start and end apart: 32, of which 20 were waited for; matrix products, arithmetic and copies ran while one was open for 2% of the time, Pallas kernels for 28%

profile of v1, /device:TPU:0, one launch (start us, length us, event | category | flops | bytes accessed | tf_op | source)
XLA Modules:
  0.0 131.9 jit_solution(867559524126474337)
XLA Ops:
  0.6 2.7 %shard_map.275 = bf16[1024,256]{1,0:T(8,128)(2,1)} custom-call(s32[1,1024]{1,0:T(1,128)} %order.1, bf16[1024,256]{1,0:T(8,128)(2,1)} %rest.1), custom_call_target="tpu_custom_call" | custom-call | tf_op jit(solution)/shard_map/pallas_call | solution.py:423
  3.4 8.4 %all-to-all-start = ((bf16[16,64,256]{2,1,0:T(8,128)(2,1)}), bf16[16,64,256]{2,1,0:T(8,128)(2,1)S(1)}, u32[]{:S(2)}, u32[]{:S(2)}) async-start(bf16[16,64,256]{2,1,0:T(8,128)(2,1)} %bitcast.68), calls=%async_computation | async-start | bytes 1048576 | tf_op jit(solution)/shard_map/all_to_all | solution.py:464
  16.2 4.7 %shard_map.276 = (s32[24]{0:T(128)S(1)}, s32[624]{0:T(1024)S(1)}, s32[32]{0:T(128)S(1)}, s32[12]{0:T(128)S(1)}, f32[16,128]{1,0:T(8,128)S(1)}, /*index=5*/f32[96,128]{1,0:T(8,128)S(1)}, f32[24,128]{1,0:T(8,128)S(1)}) custom-call(s32[1]{0:T(128)} %bitcast.3.parity, f32[3,8]{1,0:T(4,128)S(1)} %copy-done.12, s32[16]{0:T(128)S(1)} %copy-done.13, ...), custom_call_target="tpu_custom_call" | custom-call | flops 2000000000 | bytes 1000000 | tf_op jit(solution)/shard_map/pallas_call | solution.py:137
  22.5 4.3 %all-to-all-done = bf16[16,64,256]{2,1,0:T(8,128)(2,1)S(1)} async-done(((bf16[16,64,256]{2,1,0:T(8,128)(2,1)}), bf16[16,64,256]{2,1,0:T(8,128)(2,1)S(1)}, u32[]{:S(2)}, u32[]{:S(2)}) %all-to-all-start) | async-done | bytes 524320 | tf_op jit(solution)/shard_map/all_to_all | solution.py:464
  26.8 1.9 %collective-permute-done.4.refs_1_ = bf16[1024,256]{1,0:T(8,128)(2,1)S(1)} collective-permute-done((bf16[1024,256]{1,0:T(8,128)(2,1)S(1)}, bf16[1024,256]{1,0:T(8,128)(2,1)S(1)}, u32[]{:S(2)}, u32[]{:S(2)}) %collective-permute-start.4) | collective-permute-done | bytes 524320 | tf_op jit(solution)/shard_map/ppermute | solution.py:460
  29.2 2.1 %shard_map.279 = (bf16[512,256]{1,0:T(8,128)(2,1)S(1)}, bf16[512,256]{1,0:T(8,128)(2,1)S(1)}) custom-call(s32[12]{0:T(128)S(1)} %get-tuple-element.91.counts, s32[24]{0:T(128)S(1)} %get-tuple-element.93.items, bf16[1024,256]{1,0:T(8,128)(2,1)S(1)} %shard_map.278.refs_0_, bf16[1024,256]{1,0:T(8,128)(2,1)S(1)} %shard_map.277.refs_1_, s32[32,128]{1,0:T(8,128)S(1)} %bitcast.67, ...), custom_call_target="tpu_custom_call" | custom-call | flops 2000000000 | bytes 2000000 | tf_op jit(solution)/shard_map/pallas_call | solution.py:252
  40.4 2.1 %shard_map.283.refs_7_ = f32[1152,256]{1,0:T(8,128)S(1)} custom-call(s32[12]{0:T(128)S(1)} %get-tuple-element.91.counts, s32[624]{0:T(1024)S(1)} %get-tuple-element.92.items, bf16[256,256]{1,0:T(8,128)(2,1)S(1)} %get-tuple-element.106.refs_0_, bf16[256,256]{1,0:T(8,128)(2,1)S(1)} %get-tuple-element.107.refs_1_, ...), custom_call_target="tpu_custom_call" | custom-call | flops 2000000000 | bytes 2000000 | tf_op jit(solution)/shard_map/pallas_call | solution.py:252
  43.2 2.0 %shard_map.284.refs_7_ = f32[1152,256]{1,0:T(8,128)S(1)} custom-call(s32[12]{0:T(128)S(1)} %get-tuple-element.91.counts, s32[624]{0:T(1024)S(1)} %get-tuple-element.92.items, bf16[256,256]{1,0:T(8,128)(2,1)S(1)} %get-tuple-element.106.refs_0_, bf16[256,256]{1,0:T(8,128)(2,1)S(1)} %get-tuple-element.107.refs_1_, ...), custom_call_target="tpu_custom_call", output_to_operand_aliasing={{}: (9, {})} | custom-call | flops 2000000000 | bytes 2000000 | tf_op jit(solution)/shard_map/pallas_call | solution.py:252
  48.5 2.1 %collective-permute-start.13 = (bf16[256,256]{1,0:T(8,128)(2,1)S(1)}, bf16[256,256]{1,0:T(8,128)(2,1)S(1)}, u32[]{:S(2)}, u32[]{:S(2)}) collective-permute-start(bf16[256,256]{1,0:T(8,128)(2,1)S(1)} %collective-permute-done.10.refs_1_), channel_id=1, source_target_pairs={{0,4},{2,30},{4,8},{6,2},{8,12},{10,6},{12,16},{14,10},{16,20},{18... | collective-permute-start | bytes 393224 | tf_op jit(solution)/shard_map/ppermute | solution.py:472
  52.4 3.6 %shard_map.286.refs_6_ = f32[1152,256]{1,0:T(8,128)S(1)} custom-call(s32[12]{0:T(128)S(1)} %get-tuple-element.91.counts, s32[624]{0:T(1024)S(1)} %get-tuple-element.92.items, bf16[256,256]{1,0:T(8,128)(2,1)S(1)} %collective-permute-done.8.refs_0_, bf16[256,256]{1,0:T(8,128)(2,1)S(1)} %collective-permute-done.10.refs_1_, ...), custom_call_target="tpu_custom_call", output_to_operand_aliasing={{}: (9, {})} | custom-call | flops 2000000000 | bytes 2000000 | tf_op jit(solution)/shard_map/pallas_call | solution.py:252
  57.2 2.8 %collective-permute-done.13.refs_1_ = bf16[256,256]{1,0:T(8,128)(2,1)S(1)} collective-permute-done((bf16[256,256]{1,0:T(8,128)(2,1)S(1)}, bf16[256,256]{1,0:T(8,128)(2,1)S(1)}, u32[]{:S(2)}, u32[]{:S(2)}) %collective-permute-start.13) | collective-permute-done | bytes 131104 | tf_op jit(solution)/shard_map/ppermute | solution.py:472
  60.0 2.8 %collective-permute-done.12.refs_0_ = bf16[256,256]{1,0:T(8,128)(2,1)S(1)} collective-permute-done((bf16[256,256]{1,0:T(8,128)(2,1)S(1)}, bf16[256,256]{1,0:T(8,128)(2,1)S(1)}, u32[]{:S(2)}, u32[]{:S(2)}) %collective-permute-start.12) | collective-permute-done | bytes 131104 | tf_op jit(solution)/shard_map/ppermute | solution.py:472
  62.9 2.3 %shard_map.287.refs_4_ = f32[1152,256]{1,0:T(8,128)S(1)} custom-call(s32[12]{0:T(128)S(1)} %get-tuple-element.91.counts, s32[624]{0:T(1024)S(1)} %get-tuple-element.92.items, bf16[256,256]{1,0:T(8,128)(2,1)S(1)} %collective-permute-done.12.refs_0_, bf16[256,256]{1,0:T(8,128)(2,1)S(1)} %collective-permute-done.13.refs_1_, ...), custom_call_target="tpu_custom_call", output_to_operand_aliasing={{}: (8, {})} | custom-call | flops 2000000000 | bytes 2000000 | tf_op jit(solution)/shard_map/pallas_call | solution.py:252
  69.7 2.0 %collective-permute-start.21 = (bf16[256,256]{1,0:T(8,128)(2,1)S(1)}, bf16[256,256]{1,0:T(8,128)(2,1)S(1)}, u32[]{:S(2)}, u32[]{:S(2)}) collective-permute-start(bf16[256,256]{1,0:T(8,128)(2,1)S(1)} %get-tuple-element.131.refs_1_), channel_id=1, source_target_pairs={{0,2},{2,0},{4,6},{6,4},{8,10},{10,8},{12,14},{14,12},{16,18},{18,... | collective-permute-start | bytes 393224 | tf_op jit(solution)/shard_map/ppermute | solution.py:472
  72.9 1.9 %collective-permute-start.17 = (bf16[256,256]{1,0:T(8,128)(2,1)S(1)}, bf16[256,256]{1,0:T(8,128)(2,1)S(1)}, u32[]{:S(2)}, u32[]{:S(2)}) collective-permute-start(bf16[256,256]{1,0:T(8,128)(2,1)S(1)} %get-tuple-element.128.refs_3_), channel_id=1, source_target_pairs={{0,2},{2,0},{4,6},{6,4},{8,10},{10,8},{12,14},{14,12},{16,18},{18,... | collective-permute-start | bytes 393224 | tf_op jit(solution)/shard_map/ppermute | solution.py:472
  76.0 2.1 %shard_map.292.refs_7_ = f32[1152,256]{1,0:T(8,128)S(1)} custom-call(s32[12]{0:T(128)S(1)} %get-tuple-element.91.counts, s32[624]{0:T(1024)S(1)} %get-tuple-element.92.items, bf16[256,256]{1,0:T(8,128)(2,1)S(1)} %get-tuple-element.130.refs_0_, bf16[256,256]{1,0:T(8,128)(2,1)S(1)} %get-tuple-element.131.refs_1_, ...), custom_call_target="tpu_custom_call" | custom-call | flops 2000000000 | bytes 2000000 | tf_op jit(solution)/shard_map/pallas_call | solution.py:252
  78.8 2.0 %shard_map.293.refs_7_ = f32[1152,256]{1,0:T(8,128)S(1)} custom-call(s32[12]{0:T(128)S(1)} %get-tuple-element.91.counts, s32[624]{0:T(1024)S(1)} %get-tuple-element.92.items, bf16[256,256]{1,0:T(8,128)(2,1)S(1)} %get-tuple-element.130.refs_0_, bf16[256,256]{1,0:T(8,128)(2,1)S(1)} %get-tuple-element.131.refs_1_, ...), custom_call_target="tpu_custom_call", output_to_operand_aliasing={{}: (9, {})} | custom-call | flops 2000000000 | bytes 2000000 | tf_op jit(solution)/shard_map/pallas_call | solution.py:252
  85.0 3.6 %shard_map.295.refs_6_ = f32[1152,256]{1,0:T(8,128)S(1)} custom-call(s32[12]{0:T(128)S(1)} %get-tuple-element.91.counts, s32[624]{0:T(1024)S(1)} %get-tuple-element.92.items, bf16[256,256]{1,0:T(8,128)(2,1)S(1)} %collective-permute-done.19.refs_0_, bf16[256,256]{1,0:T(8,128)(2,1)S(1)} %collective-permute-done.21.refs_1_, ...), custom_call_target="tpu_custom_call", output_to_operand_aliasing={{}: (9, {})} | custom-call | flops 2000000000 | bytes 2000000 | tf_op jit(solution)/shard_map/pallas_call | solution.py:252
  88.7 4.7 %collective-permute-done.25.refs_2_ = bf16[256,256]{1,0:T(8,128)(2,1)S(1)} collective-permute-done((bf16[256,256]{1,0:T(8,128)(2,1)S(1)}, bf16[256,256]{1,0:T(8,128)(2,1)S(1)}, u32[]{:S(2)}, u32[]{:S(2)}) %collective-permute-start.25) | collective-permute-done | bytes 131104 | tf_op jit(solution)/shard_map/ppermute | solution.py:472
  93.4 2.8 %collective-permute-done.24.refs_1_ = bf16[256,256]{1,0:T(8,128)(2,1)S(1)} collective-permute-done((bf16[256,256]{1,0:T(8,128)(2,1)S(1)}, bf16[256,256]{1,0:T(8,128)(2,1)S(1)}, u32[]{:S(2)}, u32[]{:S(2)}) %collective-permute-start.24) | collective-permute-done | bytes 131104 | tf_op jit(solution)/shard_map/ppermute | solution.py:472
  96.2 2.8 %collective-permute-done.23.refs_0_ = bf16[256,256]{1,0:T(8,128)(2,1)S(1)} collective-permute-done((bf16[256,256]{1,0:T(8,128)(2,1)S(1)}, bf16[256,256]{1,0:T(8,128)(2,1)S(1)}, u32[]{:S(2)}, u32[]{:S(2)}) %collective-permute-start.23) | collective-permute-done | bytes 131104 | tf_op jit(solution)/shard_map/ppermute | solution.py:472
  99.0 2.4 %shard_map.296.refs_4_ = f32[1152,256]{1,0:T(8,128)S(1)} custom-call(s32[12]{0:T(128)S(1)} %get-tuple-element.91.counts, s32[624]{0:T(1024)S(1)} %get-tuple-element.92.items, bf16[256,256]{1,0:T(8,128)(2,1)S(1)} %collective-permute-done.23.refs_0_, bf16[256,256]{1,0:T(8,128)(2,1)S(1)} %collective-permute-done.24.refs_1_, ...), custom_call_target="tpu_custom_call", output_to_operand_aliasing={{}: (8, {})} | custom-call | flops 2000000000 | bytes 2000000 | tf_op jit(solution)/shard_map/pallas_call | solution.py:252
  106.7 2.8 %shard_map.301.am = bf16[1024,256]{1,0:T(8,128)(2,1)S(1)} custom-call(s32[12]{0:T(128)S(1)} %get-tuple-element.91.counts, s32[32]{0:T(128)S(1)} %get-tuple-element.154.items, bf16[256,256]{1,0:T(8,128)(2,1)S(1)} %get-tuple-element.155.refs_0_, bf16[256,256]{1,0:T(8,128)(2,1)S(1)} %get-tuple-element.156.refs_1_, ...), custom_call_target="tpu_custom_call" | custom-call | flops 2000000000 | bytes 2000000 | tf_op jit(solution)/shard_map/pallas_call | solution.py:252
  112.3 18.1 %all_to_all.23 = bf16[16,64,256]{2,1,0:T(8,128)(2,1)S(1)} all-to-all(bf16[16,64,256]{2,1,0:T(8,128)(2,1)S(1)} %bitcast.47), channel_id=1, replica_groups=mesh['nodes'=16,'feat'=2] {'nodes'}, dimensions={0} | all-to-all | bytes 1048576 | tf_op jit(solution)/shard_map/all_to_all | solution.py:464
  (131 shorter events, 41.4 us)
Async XLA Ops:
  3.4 23.4 %all-to-all-start = ((bf16[16,64,256]{2,1,0:T(8,128)(2,1)}), bf16[16,64,256]{2,1,0:T(8,128)(2,1)S(1)}, u32[]{:S(2)}, u32[]{:S(2)}) async-start(bf16[16,64,256]{2,1,0:T(8,128)(2,1)} %bitcast.68), calls=%async_computation | async-start | bytes 1048576 | tf_op jit(solution)/shard_map/all_to_all | solution.py:464
  11.9 9.0 %collective-permute-start = (bf16[1024,256]{1,0:T(8,128)(2,1)}, bf16[1024,256]{1,0:T(8,128)(2,1)}, u32[]{:S(2)}, u32[]{:S(2)}) collective-permute-start(bf16[1024,256]{1,0:T(8,128)(2,1)} %param.29), channel_id=1, source_target_pairs={{0,1},{1,0},{2,3},{3,2},{4,5},{5,4},{6,7},{7,6},{8,9},{9,8},{10,11... | collective-permute-start | bytes 1572872 | tf_op jit(solution)/shard_map/ppermute | solution.py:460
  12.0 10.5 %collective-permute-start.1 = (bf16[512,256]{1,0:T(8,128)(2,1)S(1)}, bf16[512,256]{1,0:T(8,128)(2,1)S(1)}, u32[]{:S(2)}, u32[]{:S(2)}) collective-permute-start(bf16[512,256]{1,0:T(8,128)(2,1)S(1)} %get-tuple-element.177.wm), channel_id=1, source_target_pairs={{0,1},{1,0},{2,3},{3,2},{4,5},{5,4},{6,7},{7,6},{8,9},{9,8},{10,11... | collective-permute-start | bytes 786440 | tf_op jit(solution)/shard_map/ppermute | solution.py:460
  12.6 9.9 %collective-permute-start.2 = (f32[1,256]{1,0:T(1,128)S(1)}, f32[1,256]{1,0:T(1,128)S(1)}, u32[]{:S(2)}, u32[]{:S(2)}) collective-permute-start(f32[1,256]{1,0:T(1,128)S(1)} %bitcast.48), channel_id=1, source_target_pairs={{0,1},{1,0},{2,3},{3,2},{4,5},{5,4},{6,7},{7,6},{8,9},{9,8},{10,11... | collective-permute-start | bytes 3080 | tf_op jit(solution)/shard_map/ppermute | solution.py:460
  12.7 9.8 %collective-permute-start.3 = (f32[2,256]{1,0:T(2,128)S(1)}, f32[2,256]{1,0:T(2,128)S(1)}, u32[]{:S(2)}, u32[]{:S(2)}) collective-permute-start(f32[2,256]{1,0:T(2,128)S(1)} %copy-done.23), channel_id=1, source_target_pairs={{0,1},{1,0},{2,3},{3,2},{4,5},{5,4},{6,7},{7,6},{8,9},{9,8},{10,11... | collective-permute-start | bytes 6152 | tf_op jit(solution)/shard_map/ppermute | solution.py:460
  34.0 6.4 %collective-permute-start.8 = (bf16[256,256]{1,0:T(8,128)(2,1)S(1)}, bf16[256,256]{1,0:T(8,128)(2,1)S(1)}, u32[]{:S(2)}, u32[]{:S(2)}) collective-permute-start(bf16[256,256]{1,0:T(8,128)(2,1)S(1)} %get-tuple-element.106.refs_0_), channel_id=1, source_target_pairs={{0,2},{2,0},{4,6},{6,4},{8,10},{10,8},{12,14},{14,12},{16,18},{18,... | collective-permute-start | bytes 393224 | tf_op jit(solution)/shard_map/ppermute | solution.py:472
  34.3 8.9 %collective-permute-start.10 = (bf16[256,256]{1,0:T(8,128)(2,1)S(1)}, bf16[256,256]{1,0:T(8,128)(2,1)S(1)}, u32[]{:S(2)}, u32[]{:S(2)}) collective-permute-start(bf16[256,256]{1,0:T(8,128)(2,1)S(1)} %get-tuple-element.107.refs_1_), channel_id=1, source_target_pairs={{0,2},{2,0},{4,6},{6,4},{8,10},{10,8},{12,14},{14,12},{16,18},{18,... | collective-permute-start | bytes 393224 | tf_op jit(solution)/shard_map/ppermute | solution.py:472
  37.2 8.9 %collective-permute-start.9 = (bf16[256,256]{1,0:T(8,128)(2,1)S(1)}, bf16[256,256]{1,0:T(8,128)(2,1)S(1)}, u32[]{:S(2)}, u32[]{:S(2)}) collective-permute-start(bf16[256,256]{1,0:T(8,128)(2,1)S(1)} %get-tuple-element.108.refs_2_), channel_id=1, source_target_pairs={{0,2},{2,0},{4,6},{6,4},{8,10},{10,8},{12,14},{14,12},{16,18},{18,... | collective-permute-start | bytes 393224 | tf_op jit(solution)/shard_map/ppermute | solution.py:472
  37.5 10.5 %collective-permute-start.6 = (bf16[256,256]{1,0:T(8,128)(2,1)S(1)}, bf16[256,256]{1,0:T(8,128)(2,1)S(1)}, u32[]{:S(2)}, u32[]{:S(2)}) collective-permute-start(bf16[256,256]{1,0:T(8,128)(2,1)S(1)} %get-tuple-element.102.refs_3_), channel_id=1, source_target_pairs={{0,2},{2,0},{4,6},{6,4},{8,10},{10,8},{12,14},{14,12},{16,18},{18,... | collective-permute-start | bytes 393224 | tf_op jit(solution)/shard_map/ppermute | solution.py:472
  48.0 8.0 %collective-permute-start.15 = (bf16[512,256]{1,0:T(8,128)(2,1)S(1)}, bf16[512,256]{1,0:T(8,128)(2,1)S(1)}, u32[]{:S(2)}, u32[]{:S(2)}) collective-permute-start(bf16[512,256]{1,0:T(8,128)(2,1)S(1)} %slice_bitcast_fusion.9), channel_id=1, source_target_pairs={{0,1},{1,0},{2,3},{3,2},{4,5},{5,4},{6,7},{7,6},{8,9},{9,8},{10,11... | collective-permute-start | bytes 786440 | tf_op jit(solution)/shard_map/ppermute | solution.py:460
  48.1 9.1 %collective-permute-start.14 = (bf16[256,256]{1,0:T(8,128)(2,1)S(1)}, bf16[256,256]{1,0:T(8,128)(2,1)S(1)}, u32[]{:S(2)}, u32[]{:S(2)}) collective-permute-start(bf16[256,256]{1,0:T(8,128)(2,1)S(1)} %collective-permute-done.9.refs_2_), channel_id=1, source_target_pairs={{0,4},{2,30},{4,8},{6,2},{8,12},{10,6},{12,16},{14,10},{16,20},{18... | collective-permute-start | bytes 393224 | tf_op jit(solution)/shard_map/ppermute | solution.py:472
  48.5 11.5 %collective-permute-start.13 = (bf16[256,256]{1,0:T(8,128)(2,1)S(1)}, bf16[256,256]{1,0:T(8,128)(2,1)S(1)}, u32[]{:S(2)}, u32[]{:S(2)}) collective-permute-start(bf16[256,256]{1,0:T(8,128)(2,1)S(1)} %collective-permute-done.10.refs_1_), channel_id=1, source_target_pairs={{0,4},{2,30},{4,8},{6,2},{8,12},{10,6},{12,16},{14,10},{16,20},{18... | collective-permute-start | bytes 393224 | tf_op jit(solution)/shard_map/ppermute | solution.py:472
  50.6 12.2 %collective-permute-start.12 = (bf16[256,256]{1,0:T(8,128)(2,1)S(1)}, bf16[256,256]{1,0:T(8,128)(2,1)S(1)}, u32[]{:S(2)}, u32[]{:S(2)}) collective-permute-start(bf16[256,256]{1,0:T(8,128)(2,1)S(1)} %collective-permute-done.8.refs_0_), channel_id=1, source_target_pairs={{0,4},{2,30},{4,8},{6,2},{8,12},{10,6},{12,16},{14,10},{16,20},{18... | collective-permute-start | bytes 393224 | tf_op jit(solution)/shard_map/ppermute | solution.py:472
  51.6 13.7 %collective-permute-start.11 = (bf16[256,256]{1,0:T(8,128)(2,1)S(1)}, bf16[256,256]{1,0:T(8,128)(2,1)S(1)}, u32[]{:S(2)}, u32[]{:S(2)}) collective-permute-start(bf16[256,256]{1,0:T(8,128)(2,1)S(1)} %collective-permute-done.6.refs_3_), channel_id=1, source_target_pairs={{0,4},{2,30},{4,8},{6,2},{8,12},{10,6},{12,16},{14,10},{16,20},{18... | collective-permute-start | bytes 393224 | tf_op jit(solution)/shard_map/ppermute | solution.py:472
  69.6 6.4 %collective-permute-start.19 = (bf16[256,256]{1,0:T(8,128)(2,1)S(1)}, bf16[256,256]{1,0:T(8,128)(2,1)S(1)}, u32[]{:S(2)}, u32[]{:S(2)}) collective-permute-start(bf16[256,256]{1,0:T(8,128)(2,1)S(1)} %get-tuple-element.130.refs_0_), channel_id=1, source_target_pairs={{0,2},{2,0},{4,6},{6,4},{8,10},{10,8},{12,14},{14,12},{16,18},{18,... | collective-permute-start | bytes 393224 | tf_op jit(solution)/shard_map/ppermute | solution.py:472
  69.7 9.2 %collective-permute-start.21 = (bf16[256,256]{1,0:T(8,128)(2,1)S(1)}, bf16[256,256]{1,0:T(8,128)(2,1)S(1)}, u32[]{:S(2)}, u32[]{:S(2)}) collective-permute-start(bf16[256,256]{1,0:T(8,128)(2,1)S(1)} %get-tuple-element.131.refs_1_), channel_id=1, source_target_pairs={{0,2},{2,0},{4,6},{6,4},{8,10},{10,8},{12,14},{14,12},{16,18},{18,... | collective-permute-start | bytes 393224 | tf_op jit(solution)/shard_map/ppermute | solution.py:472
  72.8 8.9 %collective-permute-start.20 = (bf16[256,256]{1,0:T(8,128)(2,1)S(1)}, bf16[256,256]{1,0:T(8,128)(2,1)S(1)}, u32[]{:S(2)}, u32[]{:S(2)}) collective-permute-start(bf16[256,256]{1,0:T(8,128)(2,1)S(1)} %get-tuple-element.132.refs_2_), channel_id=1, source_target_pairs={{0,2},{2,0},{4,6},{6,4},{8,10},{10,8},{12,14},{14,12},{16,18},{18,... | collective-permute-start | bytes 393224 | tf_op jit(solution)/shard_map/ppermute | solution.py:472
  72.9 10.7 %collective-permute-start.17 = (bf16[256,256]{1,0:T(8,128)(2,1)S(1)}, bf16[256,256]{1,0:T(8,128)(2,1)S(1)}, u32[]{:S(2)}, u32[]{:S(2)}) collective-permute-start(bf16[256,256]{1,0:T(8,128)(2,1)S(1)} %get-tuple-element.128.refs_3_), channel_id=1, source_target_pairs={{0,2},{2,0},{4,6},{6,4},{8,10},{10,8},{12,14},{14,12},{16,18},{18,... | collective-permute-start | bytes 393224 | tf_op jit(solution)/shard_map/ppermute | solution.py:472
  83.6 5.0 %collective-permute-start.26 = (bf16[512,256]{1,0:T(8,128)(2,1)S(1)}, bf16[512,256]{1,0:T(8,128)(2,1)S(1)}, u32[]{:S(2)}, u32[]{:S(2)}) collective-permute-start(bf16[512,256]{1,0:T(8,128)(2,1)S(1)} %slice_bitcast_fusion.5), channel_id=1, source_target_pairs={{0,1},{1,0},{2,3},{3,2},{4,5},{5,4},{6,7},{7,6},{8,9},{9,8},{10,11... | collective-permute-start | bytes 786440 | tf_op jit(solution)/shard_map/ppermute | solution.py:460
  83.8 4.9 %collective-permute-start.27 = (bf16[512,256]{1,0:T(8,128)(2,1)S(1)}, bf16[512,256]{1,0:T(8,128)(2,1)S(1)}, u32[]{:S(2)}, u32[]{:S(2)}) collective-permute-start(bf16[512,256]{1,0:T(8,128)(2,1)S(1)} %slice_bitcast_fusion.4), channel_id=1, source_target_pairs={{0,1},{1,0},{2,3},{3,2},{4,5},{5,4},{6,7},{7,6},{8,9},{9,8},{10,11... | collective-permute-start | bytes 786440 | tf_op jit(solution)/shard_map/ppermute | solution.py:460
  84.3 9.1 %collective-permute-start.25 = (bf16[256,256]{1,0:T(8,128)(2,1)S(1)}, bf16[256,256]{1,0:T(8,128)(2,1)S(1)}, u32[]{:S(2)}, u32[]{:S(2)}) collective-permute-start(bf16[256,256]{1,0:T(8,128)(2,1)S(1)} %collective-permute-done.20.refs_2_), channel_id=1, source_target_pairs={{0,4},{2,30},{4,8},{6,2},{8,12},{10,6},{12,16},{14,10},{16,20},{18... | collective-permute-start | bytes 393224 | tf_op jit(solution)/shard_map/ppermute | solution.py:472
  84.3 11.9 %collective-permute-start.24 = (bf16[256,256]{1,0:T(8,128)(2,1)S(1)}, bf16[256,256]{1,0:T(8,128)(2,1)S(1)}, u32[]{:S(2)}, u32[]{:S(2)}) collective-permute-start(bf16[256,256]{1,0:T(8,128)(2,1)S(1)} %collective-permute-done.21.refs_1_), channel_id=1, source_target_pairs={{0,4},{2,30},{4,8},{6,2},{8,12},{10,6},{12,16},{14,10},{16,20},{18... | collective-permute-start | bytes 393224 | tf_op jit(solution)/shard_map/ppermute | solution.py:472
  84.6 14.4 %collective-permute-start.23 = (bf16[256,256]{1,0:T(8,128)(2,1)S(1)}, bf16[256,256]{1,0:T(8,128)(2,1)S(1)}, u32[]{:S(2)}, u32[]{:S(2)}) collective-permute-start(bf16[256,256]{1,0:T(8,128)(2,1)S(1)} %collective-permute-done.19.refs_0_), channel_id=1, source_target_pairs={{0,4},{2,30},{4,8},{6,2},{8,12},{10,6},{12,16},{14,10},{16,20},{18... | collective-permute-start | bytes 393224 | tf_op jit(solution)/shard_map/ppermute | solution.py:472
  88.6 12.7 %collective-permute-start.22 = (bf16[256,256]{1,0:T(8,128)(2,1)S(1)}, bf16[256,256]{1,0:T(8,128)(2,1)S(1)}, u32[]{:S(2)}, u32[]{:S(2)}) collective-permute-start(bf16[256,256]{1,0:T(8,128)(2,1)S(1)} %collective-permute-done.17.refs_3_), channel_id=1, source_target_pairs={{0,4},{2,30},{4,8},{6,2},{8,12},{10,6},{12,16},{14,10},{16,20},{18... | collective-permute-start | bytes 393224 | tf_op jit(solution)/shard_map/ppermute | solution.py:472
  (32 other events, 161.9 us)

commit v2 on v1

--- a/solution.py
+++ b/solution.py
@@ -204,16 +204,15 @@
     take, offsets, weights = refs[:3]
     refs = refs[3:]
     if not first:
-        before = refs.pop(0)
-    outs = refs[: max(halves, 1)]
-    refs = refs[max(halves, 1) :]
+        refs.pop(0)
+    own_total = first and last
+    count = halves + (not own_total)
+    outs, refs = refs[:count], refs[count:]
     picks, held = refs[:2]
     refs = refs[2:]
-    acc = refs.pop(0) if last else outs[0]
+    acc = refs.pop(0) if own_total else outs[halves]
     if first:
         acc[...] = jnp.zeros_like(acc)
-    elif last:
-        acc[...] = before[...]
     send = sends[0]
     if pieces_in > 1:
         joined = refs.pop(0)
@@ -234,18 +233,17 @@
     arrays = [counts, items, *sends, take, offsets, weights]
     aliases = {}
     if not first:
-        if not last:
-            aliases = {len(arrays): 0}
+        aliases = {len(arrays): halves}
         arrays.append(before)
     full = (rows + BLOCK, columns)
     scratch = [
         pltpu.VMEM((UNROLL, BLOCK, width), BF16) for width in (2 * BLOCK, columns)
     ]
-    if last:
+    shape = [jax.ShapeDtypeStruct((rows // max(halves, 1), columns), BF16)] * halves
+    if first and last:
         scratch.append(pltpu.VMEM(full, F32))
-        shape = [jax.ShapeDtypeStruct((rows // halves, columns), BF16)] * halves
     else:
-        shape = [jax.ShapeDtypeStruct(full, F32)]
+        shape.append(jax.ShapeDtypeStruct(full, F32))
     if len(sends) > 1:
         depth = sum(x.shape[0] for x in sends)
         scratch.append(pltpu.VMEM((depth, columns), BF16))
@@ -261,7 +259,7 @@
             flops=2_000_000_000, bytes_accessed=2_000_000, transcendentals=1_000_000
         ),
     )(*arrays)
-    return list(result) if last else result[0]
+    return list(result[:halves]) if last else result[0]
 
 
 def two_dots(a, b, weights, mine, other, width):
@@ -581,15 +579,15 @@
                     total,
                     0,
                 )
+        total = edge_sum(2, 0, counts, m_list, near, *common, total, 0)
         last_round = r + 1 == ROUNDS
         sources = [(mesh_weights, (r, 2))] + [(dec_weights, (2,))] * last_round
         arrays, total = tie([w for w, _ in sources], total)
         fresh = [swap(w[index]) for w, (_, index) in zip(arrays, sources)]
-        total = edge_sum(2, 0, counts, m_list, near, *common, total, 0)
+        if chunks > 1:
+            total = edge_sum(3, length, counts, m_list, far[:-1], *common, total, 0)
         total, fresh = tie(total, fresh)
         outs_other += fresh
-        if chunks > 1:
-            total = edge_sum(3, length, counts, m_list, far[:-1], *common, total, 0)
         agg = edge_sum(4, 2 * length, counts, m_list, far[-1:], *common, total, halves)
     xm, _, send = mix_halves(
         chunks,

time: 132 us -> 131 us (level)
  waiting for transfers between devices: 31.5 us -> 29.6 us
    ppermute x16, waiting for transfers between devices: 21.9 us -> 19.9 us  [ring(): return lax.ppermute(chunk, 'nodes', pairs)]
  transfers between devices with their start and end apart: 32 -> 32, of which waited for: 20 -> 21; matrix products, arithmetic and copies ran while one was open for 2% -> 2% of each run, Pallas kernels for 28% -> 28%
where the time goes in v2:
time: 131 us; the launch traced here: 130 us
  Pallas kernels  50.8 us (39%)
  waiting for transfers between devices  29.6 us (23%)
  starting transfers between devices  25.1 us (19%)
  blocking collectives  19.1 us (15%)
  between operations  3.32 us (3%)
  local copies, waits for them, and re-layouts  2.59 us (2%)
    pallas_call x14, Pallas kernels, edge_sum(): pl.pallas_call(functools.partial(edge_kernel, where, base, len(sends), ha...  31.6 us
    ppermute x16, waiting for transfers between devices, ring(): return lax.ppermute(chunk, 'nodes', pairs)  19.9 us
    all_to_all x1, blocking collectives, exchange(): return lax.all_to_all(x, 'nodes', split_axis=0, concat_axis=0, tiled=True)  19.1 us
    ppermute x16, starting transfers between devices, ring(): return lax.ppermute(chunk, 'nodes', pairs)  13 us
    all_to_all x1, starting transfers between devices, exchange(): return lax.all_to_all(x, 'nodes', split_axis=0, concat_axis=0, tiled=True)  8.35 us
    pallas_call x6, Pallas kernels, mix(): pl.pallas_call(functools.partial(mix_kernel, chunks), out_shape=shapes, i...  6.38 us
    ppermute x15, waiting for transfers between devices, swap(): return lax.ppermute(x, 'feat', [(0, 1), (1, 0)])  5.29 us
    pallas_call x1, Pallas kernels, prepare(): pl.pallas_call(functools.partial(prepare_kernel, blocks, chunks), out_sha...  4.68 us
  transfers between devices with their start and end apart: 32, of which 21 were waited for; matrix products, arithmetic and copies ran while one was open for 2% of the time, Pallas kernels for 28%

profile of v2, /device:TPU:0, one launch (start us, length us, event | category | flops | bytes accessed | tf_op | source)
XLA Modules:
  0.0 130.5 jit_solution(13311716273547204727)
XLA Ops:
  0.6 2.7 %shard_map.275 = bf16[1024,256]{1,0:T(8,128)(2,1)} custom-call(s32[1,1024]{1,0:T(1,128)} %order.1, bf16[1024,256]{1,0:T(8,128)(2,1)} %rest.1), custom_call_target="tpu_custom_call" | custom-call | tf_op jit(solution)/shard_map/pallas_call | solution.py:421
  3.4 8.4 %all-to-all-start = ((bf16[16,64,256]{2,1,0:T(8,128)(2,1)}), bf16[16,64,256]{2,1,0:T(8,128)(2,1)S(1)}, u32[]{:S(2)}, u32[]{:S(2)}) async-start(bf16[16,64,256]{2,1,0:T(8,128)(2,1)} %bitcast.68), calls=%async_computation | async-start | bytes 1048576 | tf_op jit(solution)/shard_map/all_to_all | solution.py:462
  16.2 4.7 %shard_map.276 = (s32[24]{0:T(128)S(1)}, s32[624]{0:T(1024)S(1)}, s32[32]{0:T(128)S(1)}, s32[12]{0:T(128)S(1)}, f32[16,128]{1,0:T(8,128)S(1)}, /*index=5*/f32[96,128]{1,0:T(8,128)S(1)}, f32[24,128]{1,0:T(8,128)S(1)}) custom-call(s32[1]{0:T(128)} %bitcast.3.parity, f32[3,8]{1,0:T(4,128)S(1)} %copy-done.12, s32[16]{0:T(128)S(1)} %copy-done.13, ...), custom_call_target="tpu_custom_call" | custom-call | flops 2000000000 | bytes 1000000 | tf_op jit(solution)/shard_map/pallas_call | solution.py:137
  22.5 4.3 %all-to-all-done = bf16[16,64,256]{2,1,0:T(8,128)(2,1)S(1)} async-done(((bf16[16,64,256]{2,1,0:T(8,128)(2,1)}), bf16[16,64,256]{2,1,0:T(8,128)(2,1)S(1)}, u32[]{:S(2)}, u32[]{:S(2)}) %all-to-all-start) | async-done | bytes 524320 | tf_op jit(solution)/shard_map/all_to_all | solution.py:462
  26.8 1.9 %collective-permute-done.4.refs_1_ = bf16[1024,256]{1,0:T(8,128)(2,1)S(1)} collective-permute-done((bf16[1024,256]{1,0:T(8,128)(2,1)S(1)}, bf16[1024,256]{1,0:T(8,128)(2,1)S(1)}, u32[]{:S(2)}, u32[]{:S(2)}) %collective-permute-start.4) | collective-permute-done | bytes 524320 | tf_op jit(solution)/shard_map/ppermute | solution.py:458
  29.2 2.1 %shard_map.279 = (bf16[512,256]{1,0:T(8,128)(2,1)S(1)}, bf16[512,256]{1,0:T(8,128)(2,1)S(1)}) custom-call(s32[12]{0:T(128)S(1)} %get-tuple-element.91.counts, s32[24]{0:T(128)S(1)} %get-tuple-element.93.items, bf16[1024,256]{1,0:T(8,128)(2,1)S(1)} %shard_map.278.refs_0_, bf16[1024,256]{1,0:T(8,128)(2,1)S(1)} %shard_map.277.refs_1_, s32[32,128]{1,0:T(8,128)S(1)} %bitcast.67, ...), custom_call_target="tpu_custom_call" | custom-call | flops 2000000000 | bytes 2000000 | tf_op jit(solution)/shard_map/pallas_call | solution.py:250
  40.4 2.1 %shard_map.283.refs_7_ = f32[1152,256]{1,0:T(8,128)S(1)} custom-call(s32[12]{0:T(128)S(1)} %get-tuple-element.91.counts, s32[624]{0:T(1024)S(1)} %get-tuple-element.92.items, bf16[256,256]{1,0:T(8,128)(2,1)S(1)} %get-tuple-element.106.refs_0_, bf16[256,256]{1,0:T(8,128)(2,1)S(1)} %get-tuple-element.107.refs_1_, ...), custom_call_target="tpu_custom_call" | custom-call | flops 2000000000 | bytes 2000000 | tf_op jit(solution)/shard_map/pallas_call | solution.py:250
  43.2 2.0 %shard_map.284.refs_7_ = f32[1152,256]{1,0:T(8,128)S(1)} custom-call(s32[12]{0:T(128)S(1)} %get-tuple-element.91.counts, s32[624]{0:T(1024)S(1)} %get-tuple-element.92.items, bf16[256,256]{1,0:T(8,128)(2,1)S(1)} %get-tuple-element.106.refs_0_, bf16[256,256]{1,0:T(8,128)(2,1)S(1)} %get-tuple-element.107.refs_1_, ...), custom_call_target="tpu_custom_call", output_to_operand_aliasing={{}: (9, {})} | custom-call | flops 2000000000 | bytes 2000000 | tf_op jit(solution)/shard_map/pallas_call | solution.py:250
  48.4 2.1 %collective-permute-start.13 = (bf16[256,256]{1,0:T(8,128)(2,1)S(1)}, bf16[256,256]{1,0:T(8,128)(2,1)S(1)}, u32[]{:S(2)}, u32[]{:S(2)}) collective-permute-start(bf16[256,256]{1,0:T(8,128)(2,1)S(1)} %collective-permute-done.10.refs_1_), channel_id=1, source_target_pairs={{0,4},{2,30},{4,8},{6,2},{8,12},{10,6},{12,16},{14,10},{16,20},{18... | collective-permute-start | bytes 393224 | tf_op jit(solution)/shard_map/ppermute | solution.py:470
  51.4 3.6 %shard_map.286.refs_6_ = f32[1152,256]{1,0:T(8,128)S(1)} custom-call(s32[12]{0:T(128)S(1)} %get-tuple-element.91.counts, s32[624]{0:T(1024)S(1)} %get-tuple-element.92.items, bf16[256,256]{1,0:T(8,128)(2,1)S(1)} %collective-permute-done.8.refs_0_, bf16[256,256]{1,0:T(8,128)(2,1)S(1)} %collective-permute-done.10.refs_1_, ...), custom_call_target="tpu_custom_call", output_to_operand_aliasing={{}: (9, {})} | custom-call | flops 2000000000 | bytes 2000000 | tf_op jit(solution)/shard_map/pallas_call | solution.py:250
  55.2 1.9 %collective-permute-done.14.refs_2_ = bf16[256,256]{1,0:T(8,128)(2,1)S(1)} collective-permute-done((bf16[256,256]{1,0:T(8,128)(2,1)S(1)}, bf16[256,256]{1,0:T(8,128)(2,1)S(1)}, u32[]{:S(2)}, u32[]{:S(2)}) %collective-permute-start.14) | collective-permute-done | bytes 131104 | tf_op jit(solution)/shard_map/ppermute | solution.py:470
  57.1 2.5 %collective-permute-done.13.refs_1_ = bf16[256,256]{1,0:T(8,128)(2,1)S(1)} collective-permute-done((bf16[256,256]{1,0:T(8,128)(2,1)S(1)}, bf16[256,256]{1,0:T(8,128)(2,1)S(1)}, u32[]{:S(2)}, u32[]{:S(2)}) %collective-permute-start.13) | collective-permute-done | bytes 131104 | tf_op jit(solution)/shard_map/ppermute | solution.py:470
  61.1 2.3 %shard_map.287.refs_4_ = f32[1152,256]{1,0:T(8,128)S(1)} custom-call(s32[12]{0:T(128)S(1)} %get-tuple-element.91.counts, s32[624]{0:T(1024)S(1)} %get-tuple-element.92.items, bf16[256,256]{1,0:T(8,128)(2,1)S(1)} %collective-permute-done.12.refs_0_, bf16[256,256]{1,0:T(8,128)(2,1)S(1)} %collective-permute-done.13.refs_1_, ...), custom_call_target="tpu_custom_call", output_to_operand_aliasing={{}: (8, {})} | custom-call | flops 2000000000 | bytes 2000000 | tf_op jit(solution)/shard_map/pallas_call | solution.py:250
  68.2 2.0 %collective-permute-start.21 = (bf16[256,256]{1,0:T(8,128)(2,1)S(1)}, bf16[256,256]{1,0:T(8,128)(2,1)S(1)}, u32[]{:S(2)}, u32[]{:S(2)}) collective-permute-start(bf16[256,256]{1,0:T(8,128)(2,1)S(1)} %get-tuple-element.131.refs_1_), channel_id=1, source_target_pairs={{0,2},{2,0},{4,6},{6,4},{8,10},{10,8},{12,14},{14,12},{16,18},{18,... | collective-permute-start | bytes 393224 | tf_op jit(solution)/shard_map/ppermute | solution.py:470
  71.5 1.9 %collective-permute-start.17 = (bf16[256,256]{1,0:T(8,128)(2,1)S(1)}, bf16[256,256]{1,0:T(8,128)(2,1)S(1)}, u32[]{:S(2)}, u32[]{:S(2)}) collective-permute-start(bf16[256,256]{1,0:T(8,128)(2,1)S(1)} %get-tuple-element.128.refs_3_), channel_id=1, source_target_pairs={{0,2},{2,0},{4,6},{6,4},{8,10},{10,8},{12,14},{14,12},{16,18},{18,... | collective-permute-start | bytes 393224 | tf_op jit(solution)/shard_map/ppermute | solution.py:470
  74.6 2.1 %shard_map.292.refs_7_ = f32[1152,256]{1,0:T(8,128)S(1)} custom-call(s32[12]{0:T(128)S(1)} %get-tuple-element.91.counts, s32[624]{0:T(1024)S(1)} %get-tuple-element.92.items, bf16[256,256]{1,0:T(8,128)(2,1)S(1)} %get-tuple-element.130.refs_0_, bf16[256,256]{1,0:T(8,128)(2,1)S(1)} %get-tuple-element.131.refs_1_, ...), custom_call_target="tpu_custom_call" | custom-call | flops 2000000000 | bytes 2000000 | tf_op jit(solution)/shard_map/pallas_call | solution.py:250
  77.4 2.0 %shard_map.293.refs_7_ = f32[1152,256]{1,0:T(8,128)S(1)} custom-call(s32[12]{0:T(128)S(1)} %get-tuple-element.91.counts, s32[624]{0:T(1024)S(1)} %get-tuple-element.92.items, bf16[256,256]{1,0:T(8,128)(2,1)S(1)} %get-tuple-element.130.refs_0_, bf16[256,256]{1,0:T(8,128)(2,1)S(1)} %get-tuple-element.131.refs_1_, ...), custom_call_target="tpu_custom_call", output_to_operand_aliasing={{}: (9, {})} | custom-call | flops 2000000000 | bytes 2000000 | tf_op jit(solution)/shard_map/pallas_call | solution.py:250
  83.4 3.6 %shard_map.295.refs_6_ = f32[1152,256]{1,0:T(8,128)S(1)} custom-call(s32[12]{0:T(128)S(1)} %get-tuple-element.91.counts, s32[624]{0:T(1024)S(1)} %get-tuple-element.92.items, bf16[256,256]{1,0:T(8,128)(2,1)S(1)} %collective-permute-done.19.refs_0_, bf16[256,256]{1,0:T(8,128)(2,1)S(1)} %collective-permute-done.21.refs_1_, ...), custom_call_target="tpu_custom_call", output_to_operand_aliasing={{}: (9, {})} | custom-call | flops 2000000000 | bytes 2000000 | tf_op jit(solution)/shard_map/pallas_call | solution.py:250
  87.7 3.5 %collective-permute-done.25.refs_2_ = bf16[256,256]{1,0:T(8,128)(2,1)S(1)} collective-permute-done((bf16[256,256]{1,0:T(8,128)(2,1)S(1)}, bf16[256,256]{1,0:T(8,128)(2,1)S(1)}, u32[]{:S(2)}, u32[]{:S(2)}) %collective-permute-start.25) | collective-permute-done | bytes 131104 | tf_op jit(solution)/shard_map/ppermute | solution.py:470
  91.2 2.8 %collective-permute-done.24.refs_1_ = bf16[256,256]{1,0:T(8,128)(2,1)S(1)} collective-permute-done((bf16[256,256]{1,0:T(8,128)(2,1)S(1)}, bf16[256,256]{1,0:T(8,128)(2,1)S(1)}, u32[]{:S(2)}, u32[]{:S(2)}) %collective-permute-start.24) | collective-permute-done | bytes 131104 | tf_op jit(solution)/shard_map/ppermute | solution.py:470
  94.0 2.5 %collective-permute-done.23.refs_0_ = bf16[256,256]{1,0:T(8,128)(2,1)S(1)} collective-permute-done((bf16[256,256]{1,0:T(8,128)(2,1)S(1)}, bf16[256,256]{1,0:T(8,128)(2,1)S(1)}, u32[]{:S(2)}, u32[]{:S(2)}) %collective-permute-start.23) | collective-permute-done | bytes 131104 | tf_op jit(solution)/shard_map/ppermute | solution.py:470
  96.6 2.4 %shard_map.296.refs_4_ = f32[1152,256]{1,0:T(8,128)S(1)} custom-call(s32[12]{0:T(128)S(1)} %get-tuple-element.91.counts, s32[624]{0:T(1024)S(1)} %get-tuple-element.92.items, bf16[256,256]{1,0:T(8,128)(2,1)S(1)} %collective-permute-done.23.refs_0_, bf16[256,256]{1,0:T(8,128)(2,1)S(1)} %collective-permute-done.24.refs_1_, ...), custom_call_target="tpu_custom_call", output_to_operand_aliasing={{}: (8, {})} | custom-call | flops 2000000000 | bytes 2000000 | tf_op jit(solution)/shard_map/pallas_call | solution.py:250
  104.2 2.8 %shard_map.301.am = bf16[1024,256]{1,0:T(8,128)(2,1)S(1)} custom-call(s32[12]{0:T(128)S(1)} %get-tuple-element.91.counts, s32[32]{0:T(128)S(1)} %get-tuple-element.154.items, bf16[256,256]{1,0:T(8,128)(2,1)S(1)} %get-tuple-element.155.refs_0_, bf16[256,256]{1,0:T(8,128)(2,1)S(1)} %get-tuple-element.156.refs_1_, ...), custom_call_target="tpu_custom_call" | custom-call | flops 2000000000 | bytes 2000000 | tf_op jit(solution)/shard_map/pallas_call | solution.py:250
  109.8 19.1 %all_to_all.23 = bf16[16,64,256]{2,1,0:T(8,128)(2,1)S(1)} all-to-all(bf16[16,64,256]{2,1,0:T(8,128)(2,1)S(1)} %bitcast.47), channel_id=1, replica_groups=mesh['nodes'=16,'feat'=2] {'nodes'}, dimensions={0} | all-to-all | bytes 1048576 | tf_op jit(solution)/shard_map/all_to_all | solution.py:462
  (131 shorter events, 41.6 us)
Async XLA Ops:
  3.4 23.4 %all-to-all-start = ((bf16[16,64,256]{2,1,0:T(8,128)(2,1)}), bf16[16,64,256]{2,1,0:T(8,128)(2,1)S(1)}, u32[]{:S(2)}, u32[]{:S(2)}) async-start(bf16[16,64,256]{2,1,0:T(8,128)(2,1)} %bitcast.68), calls=%async_computation | async-start | bytes 1048576 | tf_op jit(solution)/shard_map/all_to_all | solution.py:462
  11.9 9.0 %collective-permute-start = (bf16[1024,256]{1,0:T(8,128)(2,1)}, bf16[1024,256]{1,0:T(8,128)(2,1)}, u32[]{:S(2)}, u32[]{:S(2)}) collective-permute-start(bf16[1024,256]{1,0:T(8,128)(2,1)} %param.29), channel_id=1, source_target_pairs={{0,1},{1,0},{2,3},{3,2},{4,5},{5,4},{6,7},{7,6},{8,9},{9,8},{10,11... | collective-permute-start | bytes 1572872 | tf_op jit(solution)/shard_map/ppermute | solution.py:458
  12.0 10.5 %collective-permute-start.1 = (bf16[512,256]{1,0:T(8,128)(2,1)S(1)}, bf16[512,256]{1,0:T(8,128)(2,1)S(1)}, u32[]{:S(2)}, u32[]{:S(2)}) collective-permute-start(bf16[512,256]{1,0:T(8,128)(2,1)S(1)} %get-tuple-element.177.wm), channel_id=1, source_target_pairs={{0,1},{1,0},{2,3},{3,2},{4,5},{5,4},{6,7},{7,6},{8,9},{9,8},{10,11... | collective-permute-start | bytes 786440 | tf_op jit(solution)/shard_map/ppermute | solution.py:458
  12.6 9.9 %collective-permute-start.2 = (f32[1,256]{1,0:T(1,128)S(1)}, f32[1,256]{1,0:T(1,128)S(1)}, u32[]{:S(2)}, u32[]{:S(2)}) collective-permute-start(f32[1,256]{1,0:T(1,128)S(1)} %bitcast.48), channel_id=1, source_target_pairs={{0,1},{1,0},{2,3},{3,2},{4,5},{5,4},{6,7},{7,6},{8,9},{9,8},{10,11... | collective-permute-start | bytes 3080 | tf_op jit(solution)/shard_map/ppermute | solution.py:458
  12.7 9.8 %collective-permute-start.3 = (f32[2,256]{1,0:T(2,128)S(1)}, f32[2,256]{1,0:T(2,128)S(1)}, u32[]{:S(2)}, u32[]{:S(2)}) collective-permute-start(f32[2,256]{1,0:T(2,128)S(1)} %copy-done.23), channel_id=1, source_target_pairs={{0,1},{1,0},{2,3},{3,2},{4,5},{5,4},{6,7},{7,6},{8,9},{9,8},{10,11... | collective-permute-start | bytes 6152 | tf_op jit(solution)/shard_map/ppermute | solution.py:458
  34.0 6.4 %collective-permute-start.8 = (bf16[256,256]{1,0:T(8,128)(2,1)S(1)}, bf16[256,256]{1,0:T(8,128)(2,1)S(1)}, u32[]{:S(2)}, u32[]{:S(2)}) collective-permute-start(bf16[256,256]{1,0:T(8,128)(2,1)S(1)} %get-tuple-element.106.refs_0_), channel_id=1, source_target_pairs={{0,2},{2,0},{4,6},{6,4},{8,10},{10,8},{12,14},{14,12},{16,18},{18,... | collective-permute-start | bytes 393224 | tf_op jit(solution)/shard_map/ppermute | solution.py:470
  34.3 8.9 %collective-permute-start.10 = (bf16[256,256]{1,0:T(8,128)(2,1)S(1)}, bf16[256,256]{1,0:T(8,128)(2,1)S(1)}, u32[]{:S(2)}, u32[]{:S(2)}) collective-permute-start(bf16[256,256]{1,0:T(8,128)(2,1)S(1)} %get-tuple-element.107.refs_1_), channel_id=1, source_target_pairs={{0,2},{2,0},{4,6},{6,4},{8,10},{10,8},{12,14},{14,12},{16,18},{18,... | collective-permute-start | bytes 393224 | tf_op jit(solution)/shard_map/ppermute | solution.py:470
  37.2 8.9 %collective-permute-start.9 = (bf16[256,256]{1,0:T(8,128)(2,1)S(1)}, bf16[256,256]{1,0:T(8,128)(2,1)S(1)}, u32[]{:S(2)}, u32[]{:S(2)}) collective-permute-start(bf16[256,256]{1,0:T(8,128)(2,1)S(1)} %get-tuple-element.108.refs_2_), channel_id=1, source_target_pairs={{0,2},{2,0},{4,6},{6,4},{8,10},{10,8},{12,14},{14,12},{16,18},{18,... | collective-permute-start | bytes 393224 | tf_op jit(solution)/shard_map/ppermute | solution.py:470
  37.5 10.5 %collective-permute-start.6 = (bf16[256,256]{1,0:T(8,128)(2,1)S(1)}, bf16[256,256]{1,0:T(8,128)(2,1)S(1)}, u32[]{:S(2)}, u32[]{:S(2)}) collective-permute-start(bf16[256,256]{1,0:T(8,128)(2,1)S(1)} %get-tuple-element.102.refs_3_), channel_id=1, source_target_pairs={{0,2},{2,0},{4,6},{6,4},{8,10},{10,8},{12,14},{14,12},{16,18},{18,... | collective-permute-start | bytes 393224 | tf_op jit(solution)/shard_map/ppermute | solution.py:470
  48.0 9.1 %collective-permute-start.14 = (bf16[256,256]{1,0:T(8,128)(2,1)S(1)}, bf16[256,256]{1,0:T(8,128)(2,1)S(1)}, u32[]{:S(2)}, u32[]{:S(2)}) collective-permute-start(bf16[256,256]{1,0:T(8,128)(2,1)S(1)} %collective-permute-done.9.refs_2_), channel_id=1, source_target_pairs={{0,4},{2,30},{4,8},{6,2},{8,12},{10,6},{12,16},{14,10},{16,20},{18... | collective-permute-start | bytes 393224 | tf_op jit(solution)/shard_map/ppermute | solution.py:470
  48.4 11.3 %collective-permute-start.13 = (bf16[256,256]{1,0:T(8,128)(2,1)S(1)}, bf16[256,256]{1,0:T(8,128)(2,1)S(1)}, u32[]{:S(2)}, u32[]{:S(2)}) collective-permute-start(bf16[256,256]{1,0:T(8,128)(2,1)S(1)} %collective-permute-done.10.refs_1_), channel_id=1, source_target_pairs={{0,4},{2,30},{4,8},{6,2},{8,12},{10,6},{12,16},{14,10},{16,20},{18... | collective-permute-start | bytes 393224 | tf_op jit(solution)/shard_map/ppermute | solution.py:470
  50.5 10.7 %collective-permute-start.12 = (bf16[256,256]{1,0:T(8,128)(2,1)S(1)}, bf16[256,256]{1,0:T(8,128)(2,1)S(1)}, u32[]{:S(2)}, u32[]{:S(2)}) collective-permute-start(bf16[256,256]{1,0:T(8,128)(2,1)S(1)} %collective-permute-done.8.refs_0_), channel_id=1, source_target_pairs={{0,4},{2,30},{4,8},{6,2},{8,12},{10,6},{12,16},{14,10},{16,20},{18... | collective-permute-start | bytes 393224 | tf_op jit(solution)/shard_map/ppermute | solution.py:470
  55.0 8.5 %collective-permute-start.15 = (bf16[512,256]{1,0:T(8,128)(2,1)S(1)}, bf16[512,256]{1,0:T(8,128)(2,1)S(1)}, u32[]{:S(2)}, u32[]{:S(2)}) collective-permute-start(bf16[512,256]{1,0:T(8,128)(2,1)S(1)} %slice_bitcast_fusion.9), channel_id=1, source_target_pairs={{0,1},{1,0},{2,3},{3,2},{4,5},{5,4},{6,7},{7,6},{8,9},{9,8},{10,11... | collective-permute-start | bytes 786440 | tf_op jit(solution)/shard_map/ppermute | solution.py:458
  55.1 8.7 %collective-permute-start.11 = (bf16[256,256]{1,0:T(8,128)(2,1)S(1)}, bf16[256,256]{1,0:T(8,128)(2,1)S(1)}, u32[]{:S(2)}, u32[]{:S(2)}) collective-permute-start(bf16[256,256]{1,0:T(8,128)(2,1)S(1)} %collective-permute-done.6.refs_3_), channel_id=1, source_target_pairs={{0,4},{2,30},{4,8},{6,2},{8,12},{10,6},{12,16},{14,10},{16,20},{18... | collective-permute-start | bytes 393224 | tf_op jit(solution)/shard_map/ppermute | solution.py:470
  68.1 6.4 %collective-permute-start.19 = (bf16[256,256]{1,0:T(8,128)(2,1)S(1)}, bf16[256,256]{1,0:T(8,128)(2,1)S(1)}, u32[]{:S(2)}, u32[]{:S(2)}) collective-permute-start(bf16[256,256]{1,0:T(8,128)(2,1)S(1)} %get-tuple-element.130.refs_0_), channel_id=1, source_target_pairs={{0,2},{2,0},{4,6},{6,4},{8,10},{10,8},{12,14},{14,12},{16,18},{18,... | collective-permute-start | bytes 393224 | tf_op jit(solution)/shard_map/ppermute | solution.py:470
  68.2 9.2 %collective-permute-start.21 = (bf16[256,256]{1,0:T(8,128)(2,1)S(1)}, bf16[256,256]{1,0:T(8,128)(2,1)S(1)}, u32[]{:S(2)}, u32[]{:S(2)}) collective-permute-start(bf16[256,256]{1,0:T(8,128)(2,1)S(1)} %get-tuple-element.131.refs_1_), channel_id=1, source_target_pairs={{0,2},{2,0},{4,6},{6,4},{8,10},{10,8},{12,14},{14,12},{16,18},{18,... | collective-permute-start | bytes 393224 | tf_op jit(solution)/shard_map/ppermute | solution.py:470
  71.3 8.9 %collective-permute-start.20 = (bf16[256,256]{1,0:T(8,128)(2,1)S(1)}, bf16[256,256]{1,0:T(8,128)(2,1)S(1)}, u32[]{:S(2)}, u32[]{:S(2)}) collective-permute-start(bf16[256,256]{1,0:T(8,128)(2,1)S(1)} %get-tuple-element.132.refs_2_), channel_id=1, source_target_pairs={{0,2},{2,0},{4,6},{6,4},{8,10},{10,8},{12,14},{14,12},{16,18},{18,... | collective-permute-start | bytes 393224 | tf_op jit(solution)/shard_map/ppermute | solution.py:470
  71.5 10.7 %collective-permute-start.17 = (bf16[256,256]{1,0:T(8,128)(2,1)S(1)}, bf16[256,256]{1,0:T(8,128)(2,1)S(1)}, u32[]{:S(2)}, u32[]{:S(2)}) collective-permute-start(bf16[256,256]{1,0:T(8,128)(2,1)S(1)} %get-tuple-element.128.refs_3_), channel_id=1, source_target_pairs={{0,2},{2,0},{4,6},{6,4},{8,10},{10,8},{12,14},{14,12},{16,18},{18,... | collective-permute-start | bytes 393224 | tf_op jit(solution)/shard_map/ppermute | solution.py:470
  82.2 9.1 %collective-permute-start.25 = (bf16[256,256]{1,0:T(8,128)(2,1)S(1)}, bf16[256,256]{1,0:T(8,128)(2,1)S(1)}, u32[]{:S(2)}, u32[]{:S(2)}) collective-permute-start(bf16[256,256]{1,0:T(8,128)(2,1)S(1)} %collective-permute-done.20.refs_2_), channel_id=1, source_target_pairs={{0,4},{2,30},{4,8},{6,2},{8,12},{10,6},{12,16},{14,10},{16,20},{18... | collective-permute-start | bytes 393224 | tf_op jit(solution)/shard_map/ppermute | solution.py:470
  82.2 11.9 %collective-permute-start.24 = (bf16[256,256]{1,0:T(8,128)(2,1)S(1)}, bf16[256,256]{1,0:T(8,128)(2,1)S(1)}, u32[]{:S(2)}, u32[]{:S(2)}) collective-permute-start(bf16[256,256]{1,0:T(8,128)(2,1)S(1)} %collective-permute-done.21.refs_1_), channel_id=1, source_target_pairs={{0,4},{2,30},{4,8},{6,2},{8,12},{10,6},{12,16},{14,10},{16,20},{18... | collective-permute-start | bytes 393224 | tf_op jit(solution)/shard_map/ppermute | solution.py:470
  82.9 13.7 %collective-permute-start.23 = (bf16[256,256]{1,0:T(8,128)(2,1)S(1)}, bf16[256,256]{1,0:T(8,128)(2,1)S(1)}, u32[]{:S(2)}, u32[]{:S(2)}) collective-permute-start(bf16[256,256]{1,0:T(8,128)(2,1)S(1)} %collective-permute-done.19.refs_0_), channel_id=1, source_target_pairs={{0,4},{2,30},{4,8},{6,2},{8,12},{10,6},{12,16},{14,10},{16,20},{18... | collective-permute-start | bytes 393224 | tf_op jit(solution)/shard_map/ppermute | solution.py:470
  87.1 11.9 %collective-permute-start.26 = (bf16[512,256]{1,0:T(8,128)(2,1)S(1)}, bf16[512,256]{1,0:T(8,128)(2,1)S(1)}, u32[]{:S(2)}, u32[]{:S(2)}) collective-permute-start(bf16[512,256]{1,0:T(8,128)(2,1)S(1)} %slice_bitcast_fusion.5), channel_id=1, source_target_pairs={{0,1},{1,0},{2,3},{3,2},{4,5},{5,4},{6,7},{7,6},{8,9},{9,8},{10,11... | collective-permute-start | bytes 786440 | tf_op jit(solution)/shard_map/ppermute | solution.py:458
  87.2 11.8 %collective-permute-start.27 = (bf16[512,256]{1,0:T(8,128)(2,1)S(1)}, bf16[512,256]{1,0:T(8,128)(2,1)S(1)}, u32[]{:S(2)}, u32[]{:S(2)}) collective-permute-start(bf16[512,256]{1,0:T(8,128)(2,1)S(1)} %slice_bitcast_fusion.4), channel_id=1, source_target_pairs={{0,1},{1,0},{2,3},{3,2},{4,5},{5,4},{6,7},{7,6},{8,9},{9,8},{10,11... | collective-permute-start | bytes 786440 | tf_op jit(solution)/shard_map/ppermute | solution.py:458
  91.2 7.7 %collective-permute-start.22 = (bf16[256,256]{1,0:T(8,128)(2,1)S(1)}, bf16[256,256]{1,0:T(8,128)(2,1)S(1)}, u32[]{:S(2)}, u32[]{:S(2)}) collective-permute-start(bf16[256,256]{1,0:T(8,128)(2,1)S(1)} %collective-permute-done.17.refs_3_), channel_id=1, source_target_pairs={{0,4},{2,30},{4,8},{6,2},{8,12},{10,6},{12,16},{14,10},{16,20},{18... | collective-permute-start | bytes 393224 | tf_op jit(solution)/shard_map/ppermute | solution.py:470
  (32 other events, 166.4 us)

commit v3 on v2

--- a/solution.py
+++ b/solution.py
@@ -1,4 +1,5 @@
 import functools
+import itertools
 import math
 
 import jax
@@ -13,7 +14,6 @@
 ROUNDS = 2
 UNROLL = 4
 CHUNKS = 4
-HALVES = 2
 EPSILON = 1e-05
 
 VMEM = pl.BlockSpec(memory_space=pltpu.VMEM)
@@ -41,6 +41,10 @@
 
 def list_length(slots):
     return slots + 2 * UNROLL
+
+
+def part_chunks(chunks):
+    return (1, 1, chunks - 2) if chunks > 2 else (chunks,)
 
 
 def own_parts(chunks):
@@ -199,6 +203,7 @@
 
 def edge_kernel(where, base, pieces_in, halves, first, counts, items, *refs):
     last = halves > 0
+    place = 0
     refs = list(refs)
     sends = [refs.pop(0) for _ in range(pieces_in)]
     take, offsets, weights = refs[:3]
@@ -221,12 +226,14 @@
             joined[pl.ds(k * depth, depth), :] = piece[...]
         send = joined
     edge_loop(base, counts[where], items, send, take, offsets, weights, acc, picks, held)
-    for k, out in enumerate(outs[:halves]):
+    for out in outs[:halves]:
         depth = out.shape[0]
-        out[...] = acc[pl.ds(k * depth, depth), :].astype(out.dtype)
-
-
-def edge_sum(where, base, counts, items, sends, take, offsets, weights, before, halves):
+        out[...] = acc[pl.ds(place, depth), :].astype(out.dtype)
+        place += depth
+
+
+def edge_sum(where, base, counts, items, sends, take, offsets, weights, before, parts):
+    halves = len(parts)
     last = halves > 0
     first = before is None
     rows, columns = take.shape
@@ -239,7 +246,7 @@
     scratch = [
         pltpu.VMEM((UNROLL, BLOCK, width), BF16) for width in (2 * BLOCK, columns)
     ]
-    shape = [jax.ShapeDtypeStruct((rows // max(halves, 1), columns), BF16)] * halves
+    shape = [jax.ShapeDtypeStruct((n, columns), BF16) for n in parts]
     if first and last:
         scratch.append(pltpu.VMEM(full, F32))
     else:
@@ -317,8 +324,8 @@
 def mix_halves(chunks, last, core, aggs, xms, xts, *rest):
     others = [swap(x) for x in aggs]
     results = [
-        mix(chunks // len(aggs), last, core, am, at, xm, xt, *rest)
-        for am, at, xm, xt in zip(aggs, others, xms, xts)
+        mix(n, last, core, am, at, xm, xt, *rest)
+        for n, am, at, xm, xt in zip(part_chunks(chunks), aggs, others, xms, xts)
     ]
     send = [x for _, part, _ in results for x in part]
     return [x for x, _, _ in results], [x for _, _, t in results for x in t], send
@@ -326,16 +333,17 @@
 
 def copy_kernel(*refs):
     ins, out = refs[:-1], refs[-1]
-    depth = ins[0].shape[0]
-    for k, x in enumerate(ins):
-        out[pl.ds(k * depth, depth), :] = x[...]
+    place = 0
+    for x in ins:
+        out[pl.ds(place, x.shape[0]), :] = x[...]
+        place += x.shape[0]
 
 
 def joined_rows(xs):
-    rows, width = xs[0].shape
+    rows, width = sum(x.shape[0] for x in xs), xs[0].shape[1]
     return pl.pallas_call(
         copy_kernel,
-        out_shape=jax.ShapeDtypeStruct((rows * len(xs), width), BF16),
+        out_shape=jax.ShapeDtypeStruct((rows, width), BF16),
         in_specs=[VMEM] * len(xs),
         out_specs=VMEM,
         compiler_params=params(4),
@@ -345,26 +353,26 @@
 def project_kernel(core, *refs):
     w, bias, out = refs[-3:]
     parts = len(refs[:-3]) // 2
-    depth, width = refs[0].shape
-    rows = depth * parts
-    tile = pieces(depth)
+    width = refs[0].shape[1]
+    depths = [x.shape[0] for x in refs[:parts]]
+    tile = min(pieces(n) for n in depths)
+    spots = [(k, a) for k, n in enumerate(depths) for a in range(0, n, tile)]
     mine = pl.multiple_of(core[0] * width, width)
     other = pl.multiple_of(width - core[0] * width, width)
 
-    for t in range(rows // tile):
+    for t, (which, start) in enumerate(spots):
         part = pl.ds(t * tile, tile)
-        which, inner = divmod(t * tile, depth)
-        inner = pl.ds(inner, tile)
+        inner = pl.ds(start, tile)
         xm, xt = refs[which], refs[parts + which]
         y = two_dots(xm[inner, :], xt[inner, :], w, mine, other, width)
         out[part, :] = (0.5 * (y + bias[...])).astype(BF16)
 
 
 def project(core, xm, xt, w, bias):
-    rows, width = xm[0].shape
+    rows, width = sum(x.shape[0] for x in xm), xm[0].shape[1]
     return pl.pallas_call(
         project_kernel,
-        out_shape=jax.ShapeDtypeStruct((rows * len(xm), width), BF16),
+        out_shape=jax.ShapeDtypeStruct((rows, width), BF16),
         in_specs=[SMEM] + [VMEM] * (2 * len(xm) + 2),
         out_specs=VMEM,
         compiler_params=params(),
@@ -525,9 +533,10 @@
     outs_other = [swap(outs[0])]
     gains = [enc_gain[None, :], mesh_gain]
     gains_other = [swap(x) for x in gains]
-    halves = math.gcd(HALVES, chunks)
-    xm = jnp.split(mesh_latent, halves)
-    xt = jnp.split(swap(mesh_latent), halves)
+    parts = [n * (rows // chunks) for n in part_chunks(chunks)]
+    cuts = list(itertools.accumulate(parts))[:-1]
+    xm = jnp.split(mesh_latent, cuts)
+    xt = jnp.split(swap(mesh_latent), cuts)
     take = project(core, xm, xt, enc_weights[1], enc_bias[None, :])
     arrived, prepared, take, outs_other, gains_other, xm, xt = tie(
         arrived, prepared, take, outs_other, gains_other, xm, xt
@@ -540,7 +549,7 @@
     arrived_other = swap(arrived)
     nothing = jnp.zeros((1, columns), F32)
     send = project(core, [arrived], [arrived_other], enc_weights[0], nothing)
-    agg = edge_sum(0, 0, counts, e_list, [send], take, e_off, e_w, None, halves)
+    agg = edge_sum(0, 0, counts, e_list, [send], take, e_off, e_w, None, parts)
     grid_take = project(core, [arrived], [arrived_other], dec_weights[1], dec_bias[None, :])
     for r in range(ROUNDS):
         xm, xt, send = mix_halves(
@@ -577,18 +586,18 @@
                     send,
                     *common,
                     total,
-                    0,
+                    (),
                 )
-        total = edge_sum(2, 0, counts, m_list, near, *common, total, 0)
+        total = edge_sum(2, 0, counts, m_list, near, *common, total, ())
         last_round = r + 1 == ROUNDS
         sources = [(mesh_weights, (r, 2))] + [(dec_weights, (2,))] * last_round
         arrays, total = tie([w for w, _ in sources], total)
         fresh = [swap(w[index]) for w, (_, index) in zip(arrays, sources)]
         if chunks > 1:
-            total = edge_sum(3, length, counts, m_list, far[:-1], *common, total, 0)
+            total = edge_sum(3, length, counts, m_list, far[:-1], *common, total, ())
         total, fresh = tie(total, fresh)
         outs_other += fresh
-        agg = edge_sum(4, 2 * length, counts, m_list, far[-1:], *common, total, halves)
+        agg = edge_sum(4, 2 * length, counts, m_list, far[-1:], *common, total, parts)
     xm, _, send = mix_halves(
         chunks,
         True,
@@ -602,7 +611,7 @@
         gains_other[ROUNDS],
         dec_weights[0],
     )
-    (agg,) = edge_sum(1, 0, counts, d_list, send, grid_take, d_off, d_w, None, 1)
+    (agg,) = edge_sum(1, 0, counts, d_list, send, grid_take, d_off, d_w, None, [rows])
     xm, agg = tie(xm, agg)
     other = swap(agg)
     mesh_out = joined_rows(xm)

time: 131 us -> 123 us (0.939)
  waiting for transfers between devices: 29.6 us -> 21.9 us
  local copies, waits for them, and re-layouts: 2.59 us -> 4.34 us
  starting transfers between devices: 25.1 us -> 23.5 us
    ppermute x16, waiting for transfers between devices: 19.9 us -> 14.4 us  [ring(): return lax.ppermute(chunk, 'nodes', pairs)]
    ppermute x16, starting transfers between devices: 13 us -> 11.1 us  [ring(): return lax.ppermute(chunk, 'nodes', pairs)]
    all_to_all x1, waiting for transfers between devices: 4.34 us -> 2.55 us  [exchange(): return lax.all_to_all(x, 'nodes', split_axis=0, concat_axis=0, tiled=True)]
    split x2 -> x4, local copies, waits for them, and re-layouts: 2.13 us -> 3.92 us  [the longest x2 1.96 us: local(): xm = jnp.split(mesh_latent, cuts)]
    pallas_call x6 -> x9, Pallas kernels: 6.38 us -> 7.23 us  [mix(): pl.pallas_call(functools.partial(mix_kernel, chunks), out_shape=shapes, i...]
    ppermute x15 -> x18, starting transfers between devices: 3.72 us -> 4.09 us  [swap(): return lax.ppermute(x, 'feat', [(0, 1), (1, 0)])]
    ppermute x15 -> x18, waiting for transfers between devices: 5.29 us -> 4.97 us  [swap(): return lax.ppermute(x, 'feat', [(0, 1), (1, 0)])]
  transfers between devices with their start and end apart: 32 -> 35, of which waited for: 21 -> 15; matrix products, arithmetic and copies ran while one was open for 2% -> 3% of each run, Pallas kernels for 28% -> 30%
where the time goes in v3:
time: 123 us
  Pallas kernels  51.7 us (42%)
  starting transfers between devices  23.5 us (19%)
  waiting for transfers between devices  21.9 us (18%)
  blocking collectives  18.1 us (15%)
  local copies, waits for them, and re-layouts  4.34 us (4%)
  between operations  3.42 us (3%)
    pallas_call x14, Pallas kernels, edge_sum(): pl.pallas_call(functools.partial(edge_kernel, where, base, len(sends), ha...  31.7 us
    all_to_all x1, blocking collectives, exchange(): return lax.all_to_all(x, 'nodes', split_axis=0, concat_axis=0, tiled=True)  18.1 us
    ppermute x16, waiting for transfers between devices, ring(): return lax.ppermute(chunk, 'nodes', pairs)  14.4 us
    ppermute x16, starting transfers between devices, ring(): return lax.ppermute(chunk, 'nodes', pairs)  11.1 us
    all_to_all x1, starting transfers between devices, exchange(): return lax.all_to_all(x, 'nodes', split_axis=0, concat_axis=0, tiled=True)  8.35 us
    pallas_call x9, Pallas kernels, mix(): pl.pallas_call(functools.partial(mix_kernel, chunks), out_shape=shapes, i...  7.23 us
    ppermute x18, waiting for transfers between devices, swap(): return lax.ppermute(x, 'feat', [(0, 1), (1, 0)])  4.97 us
    pallas_call x1, Pallas kernels, prepare(): pl.pallas_call(functools.partial(prepare_kernel, blocks, chunks), out_sha...  4.68 us
  transfers between devices with their start and end apart: 35, of which 15 were waited for; matrix products, arithmetic and copies ran while one was open for 3% of the time, Pallas kernels for 30%

profile of v3, /device:TPU:0, one launch (start us, length us, event | category | flops | bytes accessed | tf_op | source)
XLA Modules:
  0.0 122.9 jit_solution(17308704984013710747)
XLA Ops:
  0.6 2.7 %shard_map.275 = bf16[1024,256]{1,0:T(8,128)(2,1)} custom-call(s32[1,1024]{1,0:T(1,128)} %order.1, bf16[1024,256]{1,0:T(8,128)(2,1)} %rest.1), custom_call_target="tpu_custom_call" | custom-call | tf_op jit(solution)/shard_map/pallas_call | solution.py:429
  3.4 8.4 %all-to-all-start = ((bf16[16,64,256]{2,1,0:T(8,128)(2,1)}), bf16[16,64,256]{2,1,0:T(8,128)(2,1)S(1)}, u32[]{:S(2)}, u32[]{:S(2)}) async-start(bf16[16,64,256]{2,1,0:T(8,128)(2,1)} %bitcast.69), calls=%async_computation | async-start | bytes 1048576 | tf_op jit(solution)/shard_map/all_to_all | solution.py:470
  16.1 4.7 %shard_map.276 = (s32[24]{0:T(128)S(1)}, s32[624]{0:T(1024)S(1)}, s32[32]{0:T(128)S(1)}, s32[12]{0:T(128)S(1)}, f32[16,128]{1,0:T(8,128)S(1)}, /*index=5*/f32[96,128]{1,0:T(8,128)S(1)}, f32[24,128]{1,0:T(8,128)S(1)}) custom-call(s32[1]{0:T(128)} %bitcast.3.parity, f32[3,8]{1,0:T(4,128)S(1)} %copy-done.12, s32[16]{0:T(128)S(1)} %copy-done.13, ...), custom_call_target="tpu_custom_call" | custom-call | flops 2000000000 | bytes 1000000 | tf_op jit(solution)/shard_map/pallas_call | solution.py:141
  24.3 2.5 %all-to-all-done = bf16[16,64,256]{2,1,0:T(8,128)(2,1)S(1)} async-done(((bf16[16,64,256]{2,1,0:T(8,128)(2,1)}), bf16[16,64,256]{2,1,0:T(8,128)(2,1)S(1)}, u32[]{:S(2)}, u32[]{:S(2)}) %all-to-all-start) | async-done | bytes 524320 | tf_op jit(solution)/shard_map/all_to_all | solution.py:470
  26.8 1.9 %collective-permute-done.4.refs_1_ = bf16[1024,256]{1,0:T(8,128)(2,1)S(1)} collective-permute-done((bf16[1024,256]{1,0:T(8,128)(2,1)S(1)}, bf16[1024,256]{1,0:T(8,128)(2,1)S(1)}, u32[]{:S(2)}, u32[]{:S(2)}) %collective-permute-start.4) | collective-permute-done | bytes 524320 | tf_op jit(solution)/shard_map/ppermute | solution.py:466
  29.2 2.1 %shard_map.279 = (bf16[256,256]{1,0:T(8,128)(2,1)S(1)}, bf16[256,256]{1,0:T(8,128)(2,1)S(1)}, bf16[512,256]{1,0:T(8,128)(2,1)S(1)}) custom-call(s32[12]{0:T(128)S(1)} %get-tuple-element.102.counts, s32[24]{0:T(128)S(1)} %get-tuple-element.104.items, bf16[1024,256]{1,0:T(8,128)(2,1)S(1)} %shard_map.278.refs_0_, bf16[1024,256]{1,0:T(8,128)(2,1)S(1)} %shard_map.277.refs_1_, ...), custom_call_target="tpu_custom_call" | custom-call | flops 2000000000 | bytes 2000000 | tf_op jit(solution)/shard_map/pallas_call | solution.py:257
  34.4 1.8 %collective-permute-start.11 = (bf16[256,256]{1,0:T(8,128)(2,1)S(1)}, bf16[256,256]{1,0:T(8,128)(2,1)S(1)}, u32[]{:S(2)}, u32[]{:S(2)}) collective-permute-start(bf16[256,256]{1,0:T(8,128)(2,1)S(1)} %get-tuple-element.121.refs_1_), channel_id=1, source_target_pairs={{0,2},{2,0},{4,6},{6,4},{8,10},{10,8},{12,14},{14,12},{16,18},{18,... | collective-permute-start | bytes 393224 | tf_op jit(solution)/shard_map/ppermute | solution.py:478
  39.9 2.1 %shard_map.284.refs_7_ = f32[1152,256]{1,0:T(8,128)S(1)} custom-call(s32[12]{0:T(128)S(1)} %get-tuple-element.102.counts, s32[624]{0:T(1024)S(1)} %get-tuple-element.103.items, bf16[256,256]{1,0:T(8,128)(2,1)S(1)} %get-tuple-element.117.refs_0_, bf16[256,256]{1,0:T(8,128)(2,1)S(1)} %get-tuple-element.121.refs_1_, ...), custom_call_target="tpu_custom_call" | custom-call | flops 2000000000 | bytes 2000000 | tf_op jit(solution)/shard_map/pallas_call | solution.py:257
  43.0 2.1 %collective-permute-start.13 = (bf16[256,256]{1,0:T(8,128)(2,1)S(1)}, bf16[256,256]{1,0:T(8,128)(2,1)S(1)}, u32[]{:S(2)}, u32[]{:S(2)}) collective-permute-start(bf16[256,256]{1,0:T(8,128)(2,1)S(1)} %collective-permute-done.9.refs_0_), channel_id=1, source_target_pairs={{0,4},{2,30},{4,8},{6,2},{8,12},{10,6},{12,16},{14,10},{16,20},{18... | collective-permute-start | bytes 393224 | tf_op jit(solution)/shard_map/ppermute | solution.py:478
  45.1 2.0 %shard_map.285.refs_7_ = f32[1152,256]{1,0:T(8,128)S(1)} custom-call(s32[12]{0:T(128)S(1)} %get-tuple-element.102.counts, s32[624]{0:T(1024)S(1)} %get-tuple-element.103.items, bf16[256,256]{1,0:T(8,128)(2,1)S(1)} %get-tuple-element.117.refs_0_, bf16[256,256]{1,0:T(8,128)(2,1)S(1)} %get-tuple-element.121.refs_1_, ...), custom_call_target="tpu_custom_call", output_to_operand_aliasing={{}: (9, {})} | custom-call | flops 2000000000 | bytes 2000000 | tf_op jit(solution)/shard_map/pallas_call | solution.py:257
  49.0 3.6 %shard_map.287.refs_6_ = f32[1152,256]{1,0:T(8,128)S(1)} custom-call(s32[12]{0:T(128)S(1)} %get-tuple-element.102.counts, s32[624]{0:T(1024)S(1)} %get-tuple-element.103.items, bf16[256,256]{1,0:T(8,128)(2,1)S(1)} %collective-permute-done.9.refs_0_, bf16[256,256]{1,0:T(8,128)(2,1)S(1)} %collective-permute-done.11.refs_1_, ...), custom_call_target="tpu_custom_call", output_to_operand_aliasing={{}: (9, {})} | custom-call | flops 2000000000 | bytes 2000000 | tf_op jit(solution)/shard_map/pallas_call | solution.py:257
  52.8 3.8 %collective-permute-done.15.refs_2_ = bf16[256,256]{1,0:T(8,128)(2,1)S(1)} collective-permute-done((bf16[256,256]{1,0:T(8,128)(2,1)S(1)}, bf16[256,256]{1,0:T(8,128)(2,1)S(1)}, u32[]{:S(2)}, u32[]{:S(2)}) %collective-permute-start.15) | collective-permute-done | bytes 131104 | tf_op jit(solution)/shard_map/ppermute | solution.py:478
  56.6 2.4 %shard_map.288.refs_4_ = f32[1152,256]{1,0:T(8,128)S(1)} custom-call(s32[12]{0:T(128)S(1)} %get-tuple-element.102.counts, s32[624]{0:T(1024)S(1)} %get-tuple-element.103.items, bf16[256,256]{1,0:T(8,128)(2,1)S(1)} %collective-permute-done.13.refs_0_, bf16[256,256]{1,0:T(8,128)(2,1)S(1)} %collective-permute-done.14.refs_1_, ...), custom_call_target="tpu_custom_call", output_to_operand_aliasing={{}: (8, {})} | custom-call | flops 2000000000 | bytes 2000000 | tf_op jit(solution)/shard_map/pallas_call | solution.py:257
  59.0 2.3 %collective-permute-done.12.refs_0_ = bf16[256,256]{1,0:T(8,128)(2,1)S(1)} collective-permute-done((bf16[256,256]{1,0:T(8,128)(2,1)S(1)}, bf16[256,256]{1,0:T(8,128)(2,1)S(1)}, u32[]{:S(2)}, u32[]{:S(2)}) %collective-permute-start.12) | collective-permute-done | bytes 131104 | tf_op jit(solution)/shard_map/ppermute | solution.py:478
  66.0 2.1 %collective-permute-start.23 = (bf16[256,256]{1,0:T(8,128)(2,1)S(1)}, bf16[256,256]{1,0:T(8,128)(2,1)S(1)}, u32[]{:S(2)}, u32[]{:S(2)}) collective-permute-start(bf16[256,256]{1,0:T(8,128)(2,1)S(1)} %get-tuple-element.148.refs_1_), channel_id=1, source_target_pairs={{0,2},{2,0},{4,6},{6,4},{8,10},{10,8},{12,14},{14,12},{16,18},{18,... | collective-permute-start | bytes 393224 | tf_op jit(solution)/shard_map/ppermute | solution.py:478
  69.3 2.0 %collective-permute-start.18 = (bf16[256,256]{1,0:T(8,128)(2,1)S(1)}, bf16[256,256]{1,0:T(8,128)(2,1)S(1)}, u32[]{:S(2)}, u32[]{:S(2)}) collective-permute-start(bf16[256,256]{1,0:T(8,128)(2,1)S(1)} %get-tuple-element.144.refs_3_), channel_id=1, source_target_pairs={{0,2},{2,0},{4,6},{6,4},{8,10},{10,8},{12,14},{14,12},{16,18},{18,... | collective-permute-start | bytes 393224 | tf_op jit(solution)/shard_map/ppermute | solution.py:478
  71.7 2.1 %shard_map.294.refs_7_ = f32[1152,256]{1,0:T(8,128)S(1)} custom-call(s32[12]{0:T(128)S(1)} %get-tuple-element.102.counts, s32[624]{0:T(1024)S(1)} %get-tuple-element.103.items, bf16[256,256]{1,0:T(8,128)(2,1)S(1)} %get-tuple-element.146.refs_0_, bf16[256,256]{1,0:T(8,128)(2,1)S(1)} %get-tuple-element.148.refs_1_, ...), custom_call_target="tpu_custom_call" | custom-call | flops 2000000000 | bytes 2000000 | tf_op jit(solution)/shard_map/pallas_call | solution.py:257
  74.5 2.0 %shard_map.295.refs_7_ = f32[1152,256]{1,0:T(8,128)S(1)} custom-call(s32[12]{0:T(128)S(1)} %get-tuple-element.102.counts, s32[624]{0:T(1024)S(1)} %get-tuple-element.103.items, bf16[256,256]{1,0:T(8,128)(2,1)S(1)} %get-tuple-element.146.refs_0_, bf16[256,256]{1,0:T(8,128)(2,1)S(1)} %get-tuple-element.148.refs_1_, ...), custom_call_target="tpu_custom_call", output_to_operand_aliasing={{}: (9, {})} | custom-call | flops 2000000000 | bytes 2000000 | tf_op jit(solution)/shard_map/pallas_call | solution.py:257
  79.5 3.6 %shard_map.297.refs_6_ = f32[1152,256]{1,0:T(8,128)S(1)} custom-call(s32[12]{0:T(128)S(1)} %get-tuple-element.102.counts, s32[624]{0:T(1024)S(1)} %get-tuple-element.103.items, bf16[256,256]{1,0:T(8,128)(2,1)S(1)} %collective-permute-done.21.refs_0_, bf16[256,256]{1,0:T(8,128)(2,1)S(1)} %collective-permute-done.23.refs_1_, ...), custom_call_target="tpu_custom_call", output_to_operand_aliasing={{}: (9, {})} | custom-call | flops 2000000000 | bytes 2000000 | tf_op jit(solution)/shard_map/pallas_call | solution.py:257
  84.2 2.9 %collective-permute-done.27.refs_2_ = bf16[256,256]{1,0:T(8,128)(2,1)S(1)} collective-permute-done((bf16[256,256]{1,0:T(8,128)(2,1)S(1)}, bf16[256,256]{1,0:T(8,128)(2,1)S(1)}, u32[]{:S(2)}, u32[]{:S(2)}) %collective-permute-start.27) | collective-permute-done | bytes 131104 | tf_op jit(solution)/shard_map/ppermute | solution.py:478
  87.1 2.3 %shard_map.298.refs_4_ = f32[1152,256]{1,0:T(8,128)S(1)} custom-call(s32[12]{0:T(128)S(1)} %get-tuple-element.102.counts, s32[624]{0:T(1024)S(1)} %get-tuple-element.103.items, bf16[256,256]{1,0:T(8,128)(2,1)S(1)} %collective-permute-done.25.refs_0_, bf16[256,256]{1,0:T(8,128)(2,1)S(1)} %collective-permute-done.26.refs_1_, ...), custom_call_target="tpu_custom_call", output_to_operand_aliasing={{}: (8, {})} | custom-call | flops 2000000000 | bytes 2000000 | tf_op jit(solution)/shard_map/pallas_call | solution.py:257
  89.5 2.5 %collective-permute-done.24.refs_0_ = bf16[256,256]{1,0:T(8,128)(2,1)S(1)} collective-permute-done((bf16[256,256]{1,0:T(8,128)(2,1)S(1)}, bf16[256,256]{1,0:T(8,128)(2,1)S(1)}, u32[]{:S(2)}, u32[]{:S(2)}) %collective-permute-start.24) | collective-permute-done | bytes 131104 | tf_op jit(solution)/shard_map/ppermute | solution.py:478
  97.7 2.8 %shard_map.304.am = bf16[1024,256]{1,0:T(8,128)(2,1)S(1)} custom-call(s32[12]{0:T(128)S(1)} %get-tuple-element.102.counts, s32[32]{0:T(128)S(1)} %get-tuple-element.175.items, bf16[256,256]{1,0:T(8,128)(2,1)S(1)} %get-tuple-element.176.refs_0_, bf16[256,256]{1,0:T(8,128)(2,1)S(1)} %get-tuple-element.177.refs_1_, ...), custom_call_target="tpu_custom_call" | custom-call | flops 2000000000 | bytes 2000000 | tf_op jit(solution)/shard_map/pallas_call | solution.py:257
  103.3 18.1 %all_to_all.23 = bf16[16,64,256]{2,1,0:T(8,128)(2,1)S(1)} all-to-all(bf16[16,64,256]{2,1,0:T(8,128)(2,1)S(1)} %bitcast.47), channel_id=1, replica_groups=mesh['nodes'=16,'feat'=2] {'nodes'}, dimensions={0} | all-to-all | bytes 1048576 | tf_op jit(solution)/shard_map/all_to_all | solution.py:470
  (142 shorter events, 36.5 us)
Async XLA Ops:
  3.4 23.4 %all-to-all-start = ((bf16[16,64,256]{2,1,0:T(8,128)(2,1)}), bf16[16,64,256]{2,1,0:T(8,128)(2,1)S(1)}, u32[]{:S(2)}, u32[]{:S(2)}) async-start(bf16[16,64,256]{2,1,0:T(8,128)(2,1)} %bitcast.69), calls=%async_computation | async-start | bytes 1048576 | tf_op jit(solution)/shard_map/all_to_all | solution.py:470
  11.9 9.9 %collective-permute-start = (bf16[1024,256]{1,0:T(8,128)(2,1)}, bf16[1024,256]{1,0:T(8,128)(2,1)}, u32[]{:S(2)}, u32[]{:S(2)}) collective-permute-start(bf16[1024,256]{1,0:T(8,128)(2,1)} %param.29), channel_id=1, source_target_pairs={{0,1},{1,0},{2,3},{3,2},{4,5},{5,4},{6,7},{7,6},{8,9},{9,8},{10,11... | collective-permute-start | bytes 1572872 | tf_op jit(solution)/shard_map/ppermute | solution.py:466
  12.0 12.3 %collective-permute-start.1 = (bf16[512,256]{1,0:T(8,128)(2,1)S(1)}, bf16[512,256]{1,0:T(8,128)(2,1)S(1)}, u32[]{:S(2)}, u32[]{:S(2)}) collective-permute-start(bf16[512,256]{1,0:T(8,128)(2,1)S(1)} %get-tuple-element.199.wm), channel_id=1, source_target_pairs={{0,1},{1,0},{2,3},{3,2},{4,5},{5,4},{6,7},{7,6},{8,9},{9,8},{10,11... | collective-permute-start | bytes 786440 | tf_op jit(solution)/shard_map/ppermute | solution.py:466
  12.6 11.7 %collective-permute-start.2 = (f32[1,256]{1,0:T(1,128)S(1)}, f32[1,256]{1,0:T(1,128)S(1)}, u32[]{:S(2)}, u32[]{:S(2)}) collective-permute-start(f32[1,256]{1,0:T(1,128)S(1)} %bitcast.48), channel_id=1, source_target_pairs={{0,1},{1,0},{2,3},{3,2},{4,5},{5,4},{6,7},{7,6},{8,9},{9,8},{10,11... | collective-permute-start | bytes 3080 | tf_op jit(solution)/shard_map/ppermute | solution.py:466
  12.7 11.6 %collective-permute-start.3 = (f32[2,256]{1,0:T(2,128)S(1)}, f32[2,256]{1,0:T(2,128)S(1)}, u32[]{:S(2)}, u32[]{:S(2)}) collective-permute-start(f32[2,256]{1,0:T(2,128)S(1)} %copy-done.23), channel_id=1, source_target_pairs={{0,1},{1,0},{2,3},{3,2},{4,5},{5,4},{6,7},{7,6},{8,9},{9,8},{10,11... | collective-permute-start | bytes 6152 | tf_op jit(solution)/shard_map/ppermute | solution.py:466
  33.4 6.5 %collective-permute-start.9 = (bf16[256,256]{1,0:T(8,128)(2,1)S(1)}, bf16[256,256]{1,0:T(8,128)(2,1)S(1)}, u32[]{:S(2)}, u32[]{:S(2)}) collective-permute-start(bf16[256,256]{1,0:T(8,128)(2,1)S(1)} %get-tuple-element.117.refs_0_), channel_id=1, source_target_pairs={{0,2},{2,0},{4,6},{6,4},{8,10},{10,8},{12,14},{14,12},{16,18},{18,... | collective-permute-start | bytes 393224 | tf_op jit(solution)/shard_map/ppermute | solution.py:478
  34.4 8.2 %collective-permute-start.11 = (bf16[256,256]{1,0:T(8,128)(2,1)S(1)}, bf16[256,256]{1,0:T(8,128)(2,1)S(1)}, u32[]{:S(2)}, u32[]{:S(2)}) collective-permute-start(bf16[256,256]{1,0:T(8,128)(2,1)S(1)} %get-tuple-element.121.refs_1_), channel_id=1, source_target_pairs={{0,2},{2,0},{4,6},{6,4},{8,10},{10,8},{12,14},{14,12},{16,18},{18,... | collective-permute-start | bytes 393224 | tf_op jit(solution)/shard_map/ppermute | solution.py:478
  37.3 9.8 %collective-permute-start.10 = (bf16[256,256]{1,0:T(8,128)(2,1)S(1)}, bf16[256,256]{1,0:T(8,128)(2,1)S(1)}, u32[]{:S(2)}, u32[]{:S(2)}) collective-permute-start(bf16[256,256]{1,0:T(8,128)(2,1)S(1)} %get-tuple-element.122.refs_2_), channel_id=1, source_target_pairs={{0,2},{2,0},{4,6},{6,4},{8,10},{10,8},{12,14},{14,12},{16,18},{18,... | collective-permute-start | bytes 393224 | tf_op jit(solution)/shard_map/ppermute | solution.py:478
  37.7 11.3 %collective-permute-start.6 = (bf16[256,256]{1,0:T(8,128)(2,1)S(1)}, bf16[256,256]{1,0:T(8,128)(2,1)S(1)}, u32[]{:S(2)}, u32[]{:S(2)}) collective-permute-start(bf16[256,256]{1,0:T(8,128)(2,1)S(1)} %get-tuple-element.113.refs_3_), channel_id=1, source_target_pairs={{0,2},{2,0},{4,6},{6,4},{8,10},{10,8},{12,14},{14,12},{16,18},{18,... | collective-permute-start | bytes 393224 | tf_op jit(solution)/shard_map/ppermute | solution.py:478
  42.6 10.2 %collective-permute-start.14 = (bf16[256,256]{1,0:T(8,128)(2,1)S(1)}, bf16[256,256]{1,0:T(8,128)(2,1)S(1)}, u32[]{:S(2)}, u32[]{:S(2)}) collective-permute-start(bf16[256,256]{1,0:T(8,128)(2,1)S(1)} %collective-permute-done.11.refs_1_), channel_id=1, source_target_pairs={{0,4},{2,30},{4,8},{6,2},{8,12},{10,6},{12,16},{14,10},{16,20},{18... | collective-permute-start | bytes 393224 | tf_op jit(solution)/shard_map/ppermute | solution.py:478
  43.0 9.8 %collective-permute-start.13 = (bf16[256,256]{1,0:T(8,128)(2,1)S(1)}, bf16[256,256]{1,0:T(8,128)(2,1)S(1)}, u32[]{:S(2)}, u32[]{:S(2)}) collective-permute-start(bf16[256,256]{1,0:T(8,128)(2,1)S(1)} %collective-permute-done.9.refs_0_), channel_id=1, source_target_pairs={{0,4},{2,30},{4,8},{6,2},{8,12},{10,6},{12,16},{14,10},{16,20},{18... | collective-permute-start | bytes 393224 | tf_op jit(solution)/shard_map/ppermute | solution.py:478
  48.9 7.7 %collective-permute-start.15 = (bf16[256,256]{1,0:T(8,128)(2,1)S(1)}, bf16[256,256]{1,0:T(8,128)(2,1)S(1)}, u32[]{:S(2)}, u32[]{:S(2)}) collective-permute-start(bf16[256,256]{1,0:T(8,128)(2,1)S(1)} %collective-permute-done.10.refs_2_), channel_id=1, source_target_pairs={{0,4},{2,30},{4,8},{6,2},{8,12},{10,6},{12,16},{14,10},{16,20},{18... | collective-permute-start | bytes 393224 | tf_op jit(solution)/shard_map/ppermute | solution.py:478
  52.7 6.4 %collective-permute-start.16 = (bf16[512,256]{1,0:T(8,128)(2,1)S(1)}, bf16[512,256]{1,0:T(8,128)(2,1)S(1)}, u32[]{:S(2)}, u32[]{:S(2)}) collective-permute-start(bf16[512,256]{1,0:T(8,128)(2,1)S(1)} %slice_bitcast_fusion.9), channel_id=1, source_target_pairs={{0,1},{1,0},{2,3},{3,2},{4,5},{5,4},{6,7},{7,6},{8,9},{9,8},{10,11... | collective-permute-start | bytes 786440 | tf_op jit(solution)/shard_map/ppermute | solution.py:466
  52.7 8.6 %collective-permute-start.12 = (bf16[256,256]{1,0:T(8,128)(2,1)S(1)}, bf16[256,256]{1,0:T(8,128)(2,1)S(1)}, u32[]{:S(2)}, u32[]{:S(2)}) collective-permute-start(bf16[256,256]{1,0:T(8,128)(2,1)S(1)} %collective-permute-done.6.refs_3_), channel_id=1, source_target_pairs={{0,4},{2,30},{4,8},{6,2},{8,12},{10,6},{12,16},{14,10},{16,20},{18... | collective-permute-start | bytes 393224 | tf_op jit(solution)/shard_map/ppermute | solution.py:478
  65.2 6.5 %collective-permute-start.21 = (bf16[256,256]{1,0:T(8,128)(2,1)S(1)}, bf16[256,256]{1,0:T(8,128)(2,1)S(1)}, u32[]{:S(2)}, u32[]{:S(2)}) collective-permute-start(bf16[256,256]{1,0:T(8,128)(2,1)S(1)} %get-tuple-element.146.refs_0_), channel_id=1, source_target_pairs={{0,2},{2,0},{4,6},{6,4},{8,10},{10,8},{12,14},{14,12},{16,18},{18,... | collective-permute-start | bytes 393224 | tf_op jit(solution)/shard_map/ppermute | solution.py:478
  66.0 8.5 %collective-permute-start.23 = (bf16[256,256]{1,0:T(8,128)(2,1)S(1)}, bf16[256,256]{1,0:T(8,128)(2,1)S(1)}, u32[]{:S(2)}, u32[]{:S(2)}) collective-permute-start(bf16[256,256]{1,0:T(8,128)(2,1)S(1)} %get-tuple-element.148.refs_1_), channel_id=1, source_target_pairs={{0,2},{2,0},{4,6},{6,4},{8,10},{10,8},{12,14},{14,12},{16,18},{18,... | collective-permute-start | bytes 393224 | tf_op jit(solution)/shard_map/ppermute | solution.py:478
  69.2 8.1 %collective-permute-start.22 = (bf16[256,256]{1,0:T(8,128)(2,1)S(1)}, bf16[256,256]{1,0:T(8,128)(2,1)S(1)}, u32[]{:S(2)}, u32[]{:S(2)}) collective-permute-start(bf16[256,256]{1,0:T(8,128)(2,1)S(1)} %get-tuple-element.149.refs_2_), channel_id=1, source_target_pairs={{0,2},{2,0},{4,6},{6,4},{8,10},{10,8},{12,14},{14,12},{16,18},{18,... | collective-permute-start | bytes 393224 | tf_op jit(solution)/shard_map/ppermute | solution.py:478
  69.3 10.2 %collective-permute-start.18 = (bf16[256,256]{1,0:T(8,128)(2,1)S(1)}, bf16[256,256]{1,0:T(8,128)(2,1)S(1)}, u32[]{:S(2)}, u32[]{:S(2)}) collective-permute-start(bf16[256,256]{1,0:T(8,128)(2,1)S(1)} %get-tuple-element.144.refs_3_), channel_id=1, source_target_pairs={{0,2},{2,0},{4,6},{6,4},{8,10},{10,8},{12,14},{14,12},{16,18},{18,... | collective-permute-start | bytes 393224 | tf_op jit(solution)/shard_map/ppermute | solution.py:478
  74.5 9.3 %collective-permute-start.26 = (bf16[256,256]{1,0:T(8,128)(2,1)S(1)}, bf16[256,256]{1,0:T(8,128)(2,1)S(1)}, u32[]{:S(2)}, u32[]{:S(2)}) collective-permute-start(bf16[256,256]{1,0:T(8,128)(2,1)S(1)} %collective-permute-done.23.refs_1_), channel_id=1, source_target_pairs={{0,4},{2,30},{4,8},{6,2},{8,12},{10,6},{12,16},{14,10},{16,20},{18... | collective-permute-start | bytes 393224 | tf_op jit(solution)/shard_map/ppermute | solution.py:478
  74.5 9.7 %collective-permute-start.25 = (bf16[256,256]{1,0:T(8,128)(2,1)S(1)}, bf16[256,256]{1,0:T(8,128)(2,1)S(1)}, u32[]{:S(2)}, u32[]{:S(2)}) collective-permute-start(bf16[256,256]{1,0:T(8,128)(2,1)S(1)} %collective-permute-done.21.refs_0_), channel_id=1, source_target_pairs={{0,4},{2,30},{4,8},{6,2},{8,12},{10,6},{12,16},{14,10},{16,20},{18... | collective-permute-start | bytes 393224 | tf_op jit(solution)/shard_map/ppermute | solution.py:478
  79.5 7.7 %collective-permute-start.27 = (bf16[256,256]{1,0:T(8,128)(2,1)S(1)}, bf16[256,256]{1,0:T(8,128)(2,1)S(1)}, u32[]{:S(2)}, u32[]{:S(2)}) collective-permute-start(bf16[256,256]{1,0:T(8,128)(2,1)S(1)} %collective-permute-done.22.refs_2_), channel_id=1, source_target_pairs={{0,4},{2,30},{4,8},{6,2},{8,12},{10,6},{12,16},{14,10},{16,20},{18... | collective-permute-start | bytes 393224 | tf_op jit(solution)/shard_map/ppermute | solution.py:478
  83.1 6.4 %collective-permute-start.28 = (bf16[512,256]{1,0:T(8,128)(2,1)S(1)}, bf16[512,256]{1,0:T(8,128)(2,1)S(1)}, u32[]{:S(2)}, u32[]{:S(2)}) collective-permute-start(bf16[512,256]{1,0:T(8,128)(2,1)S(1)} %slice_bitcast_fusion.5), channel_id=1, source_target_pairs={{0,1},{1,0},{2,3},{3,2},{4,5},{5,4},{6,7},{7,6},{8,9},{9,8},{10,11... | collective-permute-start | bytes 786440 | tf_op jit(solution)/shard_map/ppermute | solution.py:466
  83.2 6.3 %collective-permute-start.29 = (bf16[512,256]{1,0:T(8,128)(2,1)S(1)}, bf16[512,256]{1,0:T(8,128)(2,1)S(1)}, u32[]{:S(2)}, u32[]{:S(2)}) collective-permute-start(bf16[512,256]{1,0:T(8,128)(2,1)S(1)} %slice_bitcast_fusion.4), channel_id=1, source_target_pairs={{0,1},{1,0},{2,3},{3,2},{4,5},{5,4},{6,7},{7,6},{8,9},{9,8},{10,11... | collective-permute-start | bytes 786440 | tf_op jit(solution)/shard_map/ppermute | solution.py:466
  83.8 8.2 %collective-permute-start.24 = (bf16[256,256]{1,0:T(8,128)(2,1)S(1)}, bf16[256,256]{1,0:T(8,128)(2,1)S(1)}, u32[]{:S(2)}, u32[]{:S(2)}) collective-permute-start(bf16[256,256]{1,0:T(8,128)(2,1)S(1)} %collective-permute-done.18.refs_3_), channel_id=1, source_target_pairs={{0,4},{2,30},{4,8},{6,2},{8,12},{10,6},{12,16},{14,10},{16,20},{18... | collective-permute-start | bytes 393224 | tf_op jit(solution)/shard_map/ppermute | solution.py:478
  (35 other events, 163.0 us)
